TPU v7x, 512 devices: a whole 4x4x16 slice. The times are simulated.
512 devices in a mesh: slab: 8 (over z_hi, y), brick: 64 (over z_lo, x, core).
Axes of the slice: x: 4, y: 4, z: 16 (z_hi: 2, z_lo: 8; z = z_hi * 8 + z_lo), core: 2. Of those that a mesh axis runs over, the one named last changes fastest.
Arguments:
- inputs: bfloat16 [256, 8, 128, 128], P('brick', None, 'slab'), may hold values from -6 to 6
- pre_first: bfloat16 [256, 8, 128, 128], P('brick', None, 'slab'), may hold values from -8 to 8
- occupancy: int32 [256, 8, 128], P('brick', None, 'slab'), may hold values 0 or 1
- grad_out: bfloat16 [256, 8, 128, 128], P('brick', None, 'slab'), may hold values from -6 to 6
- w_first: bfloat16 [27, 128, 128], replicated, may hold values from -0.109375 to 0.109375
- w_second: bfloat16 [27, 128, 128], replicated, may hold values from -0.109375 to 0.109375
Outputs:
- grad_in: bfloat16 [256, 8, 128, 128], P('brick', None, 'slab')
- grad_first: bfloat16 [27, 128, 128], replicated
- grad_second: bfloat16 [27, 128, 128], replicated
All inputs are finite; a program needn't handle non-finite values. No bound on the sum of `occupancy` on one device may be relied on, other than what follows from the above.
Results may differ from a plain program's by a relative error of at most 0.0053.
Values may be sent and summed in bfloat16 or wider, within the bound.
A program may use at most 64 MiB of HBM per device.

v0:
```python
import jax
import jax.numpy as jnp
from jax import lax
from jax.sharding import PartitionSpec as P


def with_halo(shard, sides, width):
    for axis, dim in sides:
        size, length = (lax.axis_size(axis), shard.shape[dim])
        up = [(i, (i + 1) % size) for i in range(size)]
        down = [(j, i) for i, j in up]
        last = lax.slice_in_dim(shard, length - width, length, axis=dim)
        initial = lax.slice_in_dim(shard, 0, width, axis=dim)
        before = lax.ppermute(last, axis, up)
        after = lax.ppermute(initial, axis, down)
        shard = jnp.concatenate([before, shard, after], axis=dim)
    return shard


def extend(field):
    padded = with_halo(field, (("slab", 2), ("brick", 0)), 1)
    return jnp.concatenate([padded[:, -1:], padded, padded[:, :1]], axis=1)


def columns(field):
    size_x, size_y, size_z, chans = field.shape
    padded = extend(field)
    pieces = []
    for a in (-1, 0, 1):
        for b in (-1, 0, 1):
            for c in (-1, 0, 1):
                pieces.append(
                    padded[1 - a : 1 - a + size_x, 1 - b : 1 - b + size_y, 1 - c : 1 - c + size_z]
                )
    stacked = jnp.concatenate(pieces, axis=-1)
    return stacked.reshape(size_x * size_y * size_z, 27 * chans)


def stacked_kernel(kernel):
    chans = kernel.shape[1]
    return jnp.transpose(kernel, (0, 2, 1)).reshape(27 * chans, chans)


def local_term(left, cols, scale):
    chans = left.shape[-1]
    flat_left = left.reshape(-1, chans)
    term = lax.dot_general(
        flat_left, cols, (((0,), (0,)), ((), ())), preferred_element_type=jnp.float32
    )
    term = term.reshape(chans, 27, chans).transpose(1, 0, 2)
    return term * scale


def reduce_kernel(term):
    return lax.psum(term, ("slab", "brick")).astype(jnp.bfloat16)


def per_device(inputs, pre_first, occupancy, grad_out, w_first, w_second):
    size_x, size_y, size_z, chans = inputs.shape
    cells_all = size_x * lax.axis_size("brick") * size_y * size_z * lax.axis_size("slab")
    scale = 10.0 / jnp.sqrt(jnp.float32(cells_all))
    occ = occupancy.astype(jnp.float32)[..., None]
    pre = pre_first.astype(jnp.float32)
    sig = jax.nn.sigmoid(pre)
    act = (pre * sig * occ).astype(jnp.bfloat16)
    grad_second_pre = (grad_out.astype(jnp.float32) * occ).astype(jnp.bfloat16)
    cols_second = columns(grad_second_pre)
    grad_act = jnp.dot(cols_second, stacked_kernel(w_second), preferred_element_type=jnp.float32)
    grad_act = grad_act.reshape(inputs.shape)
    second_term = local_term(act, cols_second, scale)
    grad_second = reduce_kernel(second_term)
    grad_first_pre = (grad_act * occ * sig * (1.0 + pre * (1.0 - sig))).astype(jnp.bfloat16)
    cols_first = columns(grad_first_pre)
    back = jnp.dot(cols_first, stacked_kernel(w_first), preferred_element_type=jnp.float32)
    grad_in = (grad_out.astype(jnp.float32) + back.reshape(inputs.shape)).astype(jnp.bfloat16)
    first_term = local_term(inputs, cols_first, scale)
    grad_first = reduce_kernel(first_term)
    return (grad_in, grad_first, grad_second)


def solution(mesh):
    in_specs = (
        P("brick", None, "slab", None),
        P("brick", None, "slab", None),
        P("brick", None, "slab"),
        P("brick", None, "slab", None),
        P(),
        P(),
    )
    out_specs = (P("brick", None, "slab", None), P(), P())
    return jax.shard_map(
        per_device, mesh=mesh, in_specs=in_specs, out_specs=out_specs, check_vma=False
    )
```

profile of v0, /device:TPU:1, one launch (start us, length us, event | category | flops | bytes accessed | tf_op | source)
XLA Modules:
  0.0 282.5 jit_solution(6743631901355861717)
XLA Ops:
  0.6 0.8 convert_element_type.29
  1.4 1.1 fusion.15
  2.6 4.0 %collective-permute-start = (bf16[4,8,1,128]{3,2,1,0:T(2,128)(2,1)S(1)}, bf16[4,8,1,128]{3,2,1,0:T(2,128)(2,1)S(1)}, u32[]{:S(2)}, u32[]{:S(2)}) collective-permute-start(bf16[4,8,1,128]{3,2,1,0:T(2,128)(2,1)S(1)} %get-tuple-element.15), channel_id=1, source_target_pairs={{0,64},{64,128},{128,192},{192,256},{256,320},{320,384},{384,448},... | collective-permute-start | bytes 24584 | tf_op jit(solution)/shard_map/ppermute | solution.py:14
  6.6 16.6 %collective-permute-start.1 = (bf16[4,8,1,128]{3,2,1,0:T(2,128)(2,1)S(1)}, bf16[4,8,1,128]{3,2,1,0:T(2,128)(2,1)S(1)}, u32[]{:S(2)}, u32[]{:S(2)}) collective-permute-start(bf16[4,8,1,128]{3,2,1,0:T(2,128)(2,1)S(1)} %get-tuple-element.16), channel_id=1, source_target_pairs={{64,0},{128,64},{192,128},{256,192},{320,256},{384,320},{448,384},... | collective-permute-start | bytes 24584 | tf_op jit(solution)/shard_map/ppermute | solution.py:15
  23.2 0.8 collective-permute-done.1
  24.1 4.5 %collective-permute-start.2 = (bf16[1,8,18,128]{3,2,1,0:T(8,128)(2,1)S(1)}, bf16[1,8,18,128]{3,2,1,0:T(8,128)(2,1)S(1)}, u32[]{:S(2)}, u32[]{:S(2)}) collective-permute-start(bf16[1,8,18,128]{3,2,1,0:T(8,128)(2,1)S(1)} %get-tuple-element.11), channel_id=1, source_target_pairs={{0,1},{1,2},{2,3},{3,4},{4,5},{5,6},{6,7},{7,8},{8,9},{9,10},{10,1... | collective-permute-start | bytes 110600 | tf_op jit(solution)/shard_map/ppermute | solution.py:14
  28.6 2.7 collective-permute-start.3
  31.4 1.9 copy.12
  33.3 0.8 collective-permute-done.3
  34.3 0.2 maximum_maximum_fusion
  36.1 1.8 copy-done.1
  37.9 1.1 fusion.3
  39.1 1.9 collective-permute-start.4
  41.0 14.7 %collective-permute-start.5 = (bf16[4,8,1,128]{3,2,1,0:T(2,128)(2,1)S(1)}, bf16[4,8,1,128]{3,2,1,0:T(2,128)(2,1)S(1)}, u32[]{:S(2)}, u32[]{:S(2)}) collective-permute-start(bf16[4,8,1,128]{3,2,1,0:T(2,128)(2,1)S(1)} %get-tuple-element.14), channel_id=1, source_target_pairs={{64,0},{128,64},{192,128},{256,192},{320,256},{384,320},{448,384},... | collective-permute-start | bytes 24584 | tf_op jit(solution)/shard_map/ppermute | solution.py:15
  55.8 1.3 copy.13
  57.1 5.8 %copy.15 = bf16[3456,512]{1,0:T(8,128)(2,1)} copy(bf16[3456,512]{0,1:T(8,128)(2,1)} %bitcast.43) | data formatting | bytes 7077888 | tf_op jit(solution)/shard_map/dot_general | solution.py:47
  62.9 2.4 collective-permute-start.6
  65.3 11.5 %collective-permute-start.7 = (bf16[1,8,18,128]{3,2,1,0:T(8,128)(2,1)S(1)}, bf16[1,8,18,128]{3,2,1,0:T(8,128)(2,1)S(1)}, u32[]{:S(2)}, u32[]{:S(2)}) collective-permute-start(bf16[1,8,18,128]{3,2,1,0:T(8,128)(2,1)S(1)} %get-tuple-element.8), channel_id=1, source_target_pairs={{1,0},{2,1},{3,2},{4,3},{5,4},{6,5},{7,6},{8,7},{9,8},{10,9},{11,1... | collective-permute-start | bytes 110600 | tf_op jit(solution)/shard_map/ppermute | solution.py:15
  76.8 4.3 %multiply_bitcast_fusion = f32[27,128,128]{2,1,0:T(8,128)} fusion(bf16[512,128,1]{1,0,2:T(8,128)(2,1)S(1)} %bitcast.47, bf16[27,128,512]{2,1,0:T(8,128)(2,1)} %bitcast.41), kind=kOutput, calls=%fused_computation.2 | convolution fusion | flops 453427200 | bytes 5439488 | tf_op jit(solution)/shard_map/dot_general | solution.py:47
  81.4 0.2 maximum_maximum_fusion.1
  83.2 1.8 fusion.4
  84.9 2.4 fusion
  87.3 2.2 copy.14
  89.5 193.0 %all-reduce.2 = (bf16[27,128,128]{2,1,0:T(8,128)(2,1)}, bf16[27,128,128]{2,1,0:T(8,128)(2,1)}) all-reduce(f32[27,128,128]{2,1,0:T(8,128)S(1)} %bitcast.42, f32[27,128,128]{2,1,0:T(8,128)} %multiply_bitcast_fusion), channel_id=1, replica_groups=mesh['slab'=8,'brick'=64] {'slab','brick'}, use_global_device_ids=true, to_apply=%region_0.0 | all-reduce | flops 884736 | bytes 5308416 | tf_op jit(solution)/shard_map/psum | solution.py:55
  (77 shorter events, 3.6 us)
Async XLA Ops:
  0.6 84.3 %copy-start = (bf16[4,8,16,128]{3,2,1,0:T(8,128)(2,1)S(1)}, bf16[4,8,16,128]{3,2,1,0:T(8,128)(2,1)}, u32[]{:S(2)}) copy-start(bf16[4,8,16,128]{3,2,1,0:T(8,128)(2,1)} %param.6) | copy-start | bytes 393220
  2.6 20.6 %collective-permute-start = (bf16[4,8,1,128]{3,2,1,0:T(2,128)(2,1)S(1)}, bf16[4,8,1,128]{3,2,1,0:T(2,128)(2,1)S(1)}, u32[]{:S(2)}, u32[]{:S(2)}) collective-permute-start(bf16[4,8,1,128]{3,2,1,0:T(2,128)(2,1)S(1)} %get-tuple-element.15), channel_id=1, source_target_pairs={{0,64},{64,128},{128,192},{192,256},{256,320},{320,384},{384,448},... | collective-permute-start | bytes 24584 | tf_op jit(solution)/shard_map/ppermute | solution.py:14
  6.6 17.5 %collective-permute-start.1 = (bf16[4,8,1,128]{3,2,1,0:T(2,128)(2,1)S(1)}, bf16[4,8,1,128]{3,2,1,0:T(2,128)(2,1)S(1)}, u32[]{:S(2)}, u32[]{:S(2)}) collective-permute-start(bf16[4,8,1,128]{3,2,1,0:T(2,128)(2,1)S(1)} %get-tuple-element.16), channel_id=1, source_target_pairs={{64,0},{128,64},{192,128},{256,192},{320,256},{384,320},{448,384},... | collective-permute-start | bytes 24584 | tf_op jit(solution)/shard_map/ppermute | solution.py:15
  24.1 9.2 %collective-permute-start.2 = (bf16[1,8,18,128]{3,2,1,0:T(8,128)(2,1)S(1)}, bf16[1,8,18,128]{3,2,1,0:T(8,128)(2,1)S(1)}, u32[]{:S(2)}, u32[]{:S(2)}) collective-permute-start(bf16[1,8,18,128]{3,2,1,0:T(8,128)(2,1)S(1)} %get-tuple-element.11), channel_id=1, source_target_pairs={{0,1},{1,2},{2,3},{3,4},{4,5},{5,6},{6,7},{7,8},{8,9},{9,10},{10,1... | collective-permute-start | bytes 110600 | tf_op jit(solution)/shard_map/ppermute | solution.py:14
  28.6 5.4 %collective-permute-start.3 = (bf16[1,8,18,128]{3,2,1,0:T(8,128)(2,1)S(1)}, bf16[1,8,18,128]{3,2,1,0:T(8,128)(2,1)S(1)}, u32[]{:S(2)}, u32[]{:S(2)}) collective-permute-start(bf16[1,8,18,128]{3,2,1,0:T(8,128)(2,1)S(1)} %get-tuple-element.12), channel_id=1, source_target_pairs={{1,0},{2,1},{3,2},{4,3},{5,4},{6,5},{7,6},{8,7},{9,8},{10,9},{11,1... | collective-permute-start | bytes 110600 | tf_op jit(solution)/shard_map/ppermute | solution.py:15
  34.5 3.4 %copy-start.3 = (bf16[4,8,16,128]{3,2,1,0:T(8,128)(2,1)S(1)}, bf16[4,8,16,128]{3,2,1,0:T(8,128)(2,1)}, u32[]{:S(2)}) copy-start(bf16[4,8,16,128]{3,2,1,0:T(8,128)(2,1)} %param.7) | copy-start | bytes 393220
  35.9 19.8 %copy-start.2 = (bf16[27,128,128]{2,1,0:T(8,128)(2,1)S(1)}, bf16[27,128,128]{2,1,0:T(8,128)(2,1)}, u32[]{:S(2)}) copy-start(bf16[27,128,128]{2,1,0:T(8,128)(2,1)} %param.10) | copy-start | bytes 2654212
  36.1 1.8 copy-start.1
  39.1 23.8 %collective-permute-start.4 = (bf16[4,8,1,128]{3,2,1,0:T(2,128)(2,1)S(1)}, bf16[4,8,1,128]{3,2,1,0:T(2,128)(2,1)S(1)}, u32[]{:S(2)}, u32[]{:S(2)}) collective-permute-start(bf16[4,8,1,128]{3,2,1,0:T(2,128)(2,1)S(1)} %get-tuple-element.13), channel_id=1, source_target_pairs={{0,64},{64,128},{128,192},{192,256},{256,320},{320,384},{384,448},... | collective-permute-start | bytes 24584 | tf_op jit(solution)/shard_map/ppermute | solution.py:14
  41.0 21.9 %collective-permute-start.5 = (bf16[4,8,1,128]{3,2,1,0:T(2,128)(2,1)S(1)}, bf16[4,8,1,128]{3,2,1,0:T(2,128)(2,1)S(1)}, u32[]{:S(2)}, u32[]{:S(2)}) collective-permute-start(bf16[4,8,1,128]{3,2,1,0:T(2,128)(2,1)S(1)} %get-tuple-element.14), channel_id=1, source_target_pairs={{64,0},{128,64},{192,128},{256,192},{320,256},{384,320},{448,384},... | collective-permute-start | bytes 24584 | tf_op jit(solution)/shard_map/ppermute | solution.py:15
  62.9 18.2 %collective-permute-start.6 = (bf16[1,8,18,128]{3,2,1,0:T(8,128)(2,1)S(1)}, bf16[1,8,18,128]{3,2,1,0:T(8,128)(2,1)S(1)}, u32[]{:S(2)}, u32[]{:S(2)}) collective-permute-start(bf16[1,8,18,128]{3,2,1,0:T(8,128)(2,1)S(1)} %get-tuple-element.7), channel_id=1, source_target_pairs={{0,1},{1,2},{2,3},{3,4},{4,5},{5,6},{6,7},{7,8},{8,9},{9,10},{10,1... | collective-permute-start | bytes 110600 | tf_op jit(solution)/shard_map/ppermute | solution.py:14
  65.3 15.8 %collective-permute-start.7 = (bf16[1,8,18,128]{3,2,1,0:T(8,128)(2,1)S(1)}, bf16[1,8,18,128]{3,2,1,0:T(8,128)(2,1)S(1)}, u32[]{:S(2)}, u32[]{:S(2)}) collective-permute-start(bf16[1,8,18,128]{3,2,1,0:T(8,128)(2,1)S(1)} %get-tuple-element.8), channel_id=1, source_target_pairs={{1,0},{2,1},{3,2},{4,3},{5,4},{6,5},{7,6},{8,7},{9,8},{10,9},{11,1... | collective-permute-start | bytes 110600 | tf_op jit(solution)/shard_map/ppermute | solution.py:15
  81.6 1.6 copy-start.4
where the time goes:
time: 283 us; the launch traced here: 282 us
  blocking collectives  193 us (68%)
  starting transfers between devices  58.4 us (21%)
  local copies, waits for them, and re-layouts  15.6 us (6%)
  matrix products  9.58 us (3%)
  other arithmetic  3.13 us (1%)
    psum x1, blocking collectives, reduce_kernel(): return lax.psum(term, ('slab', 'brick')).astype(jnp.bfloat16)  193 us
    ppermute x4, starting transfers between devices, with_halo(): after = lax.ppermute(initial, axis, down)  45.6 us
    ppermute x4, starting transfers between devices, with_halo(): before = lax.ppermute(last, axis, up)  12.8 us
    unnamed x60, local copies, waits for them, and re-layouts  7.56 us
    dot_general x2, matrix products, local_term(): lax.dot_general(flat_left, cols, (((0,), (0,)), ((), ())), preferred_elem...  6.73 us
    dot_general x1, local copies, waits for them, and re-layouts, local_term(): lax.dot_general(flat_left, cols, (((0,), (0,)), ((), ())), preferred_elem...  5.77 us
  transfers between devices with their start and end apart: 8, of which 2 were waited for; matrix products, arithmetic and copies ran while one was open for 5% of the time, Pallas kernels for 0%

commit v1 on v0

--- a/solution.py
+++ b/solution.py
@@ -1,6 +1,8 @@
 import jax
 import jax.numpy as jnp
 from jax import lax
+from jax.experimental import pallas as pl
+from jax.experimental.pallas import tpu as pltpu
 from jax.sharding import PartitionSpec as P
 
 
@@ -41,24 +43,174 @@
     return jnp.transpose(kernel, (0, 2, 1)).reshape(27 * chans, chans)
 
 
-def local_term(left, cols, scale):
+def local_term(left, cols):
     chans = left.shape[-1]
     flat_left = left.reshape(-1, chans)
     term = lax.dot_general(
         flat_left, cols, (((0,), (0,)), ((), ())), preferred_element_type=jnp.float32
     )
-    term = term.reshape(chans, 27, chans).transpose(1, 0, 2)
-    return term * scale
-
-
-def reduce_kernel(term):
-    return lax.psum(term, ("slab", "brick")).astype(jnp.bfloat16)
+    return term.reshape(chans, 27, chans).transpose(1, 0, 2)
+
+
+ROWS, PADDED, PIECE, TILE, SIDE, DEPTH = 432, 448, 112, 16, 4, 16
+
+
+def coordinates():
+    slab, brick = lax.axis_index("slab"), lax.axis_index("brick")
+    return (brick // 2) % 4, slab % 4, (slab // 4) * 8 + brick // 8, brick % 2
+
+
+def device(x, y, z, core):
+    return ((z // 8) * 4 + y, (z % 8) * 8 + x * 2 + core)
+
+
+def reduce_body(scale, part, out, pair, summed, first_in, second_out, second_in, tiles, deep_in, final, sems):
+    x, y, z, core = coordinates()
+    pair_s, pair_r, first_s, first_r, second_s, second_r, deep_s, deep_r, back_s, back_r = sems[:10]
+    up2_s, up2_r, up1_s, up1_r, last_s, last_r = sems[10:]
+    partner = device(x, y, z, 1 - core)
+    own = (x, y)
+
+    def peer(axis, d):
+        if axis == 0:
+            return device((x + d) % SIDE, y, z, core)
+        return device(x, (y + d) % SIDE, z, core)
+
+    def deep(d):
+        return device(x, y, (z + d) % DEPTH, core)
+
+    def send(src, dst, s, r, to):
+        return pltpu.make_async_remote_copy(
+            src_ref=src, dst_ref=dst, send_sem=s, recv_sem=r, device_id=to,
+            device_id_type=pl.DeviceIdType.MESH,
+        )
+
+    barrier = pltpu.get_barrier_semaphore()
+    everyone = [partner] + [peer(h, d) for h in (0, 1) for d in (1, 2, 3)] + [deep(d) for d in range(1, DEPTH)]
+    for to in everyone:
+        pl.semaphore_signal(barrier, inc=1, device_id=to, device_id_type=pl.DeviceIdType.MESH)
+    pl.semaphore_wait(barrier, len(everyone))
+
+    order = (2, 1, 3, 0)
+    pairs = {}
+    for d in order:
+        for h in (0, 1):
+            slot = (own[h] + d) % SIDE
+            pairs[h, d] = send(part.at[1 - core, h, slot], pair.at[h, slot], pair_s.at[h, d], pair_r.at[h, d], partner)
+            pairs[h, d].start()
+    firsts = {}
+    for d in order:
+        for h in (0, 1):
+            slot = (own[h] + d) % SIDE
+            pairs[h, d].wait_recv()
+            total = part[core, h, slot].astype(jnp.float32) + pair[h, slot].astype(jnp.float32)
+            summed[h, slot] = total.astype(jnp.bfloat16)
+            if d:
+                firsts[h, d] = send(summed.at[h, slot], first_in.at[h, d - 1], first_s.at[h, d - 1], first_r.at[h, d - 1], peer(h, d))
+                firsts[h, d].start()
+    seconds = {}
+    for h in (0, 1):
+        for d in (1, 2, 3):
+            firsts[h, d].wait_recv()
+        total = summed[h, own[h]].astype(jnp.float32)
+        for d in (1, 2, 3):
+            total = total + first_in[h, d - 1].astype(jnp.float32)
+        second_out[h] = total.astype(jnp.bfloat16).reshape(SIDE, PIECE, 128)
+        for d in (2, 1, 3):
+            slot = (own[1 - h] + d) % SIDE
+            seconds[h, d] = send(second_out.at[h, slot], second_in.at[h, d - 1], second_s.at[h, d - 1], second_r.at[h, d - 1], peer(1 - h, d))
+            seconds[h, d].start()
+    tiles[14:16] = jnp.zeros((2, TILE, 128), jnp.bfloat16)
+    for h in (0, 1):
+        for d in (1, 2, 3):
+            seconds[h, d].wait_recv()
+        total = second_out[h, own[1 - h]].astype(jnp.float32)
+        for d in (1, 2, 3):
+            total = total + second_in[h, d - 1].astype(jnp.float32)
+        tiles[7 * h : 7 * h + 7] = total.astype(jnp.bfloat16).reshape(7, TILE, 128)
+    far = sorted(range(1, DEPTH), key=lambda d: -min(d, DEPTH - d))
+    deeps = {}
+    for d in far:
+        deeps[d] = send(tiles.at[(z + d) % DEPTH], deep_in.at[d - 1], deep_s.at[d - 1], deep_r.at[d - 1], deep(d))
+        deeps[d].start()
+    total = tiles[z].astype(jnp.float32)
+    for d in reversed(far):
+        deeps[d].wait_recv()
+        total = total + deep_in[d - 1].astype(jnp.float32)
+    final[z] = (total * scale).astype(jnp.bfloat16)
+    backs = {}
+    for d in far:
+        backs[d] = send(final.at[z], final.at[z], back_s.at[d - 1], back_r.at[d - 1], deep(d))
+        backs[d].start()
+    for d in reversed(far):
+        backs[d].wait_recv()
+    up2 = {}
+    for h in (0, 1):
+        rows = pl.ds(pl.multiple_of(own[1 - h] * PIECE, PIECE), PIECE)
+        out[core, h, own[h], rows] = final[7 * h : 7 * h + 7].reshape(PIECE, 128)
+        place = out.at[core, h, own[h], rows]
+        for d in (2, 1, 3):
+            up2[h, d] = send(place, place, up2_s.at[h, d - 1], up2_r.at[h, d - 1], peer(1 - h, d))
+            up2[h, d].start()
+    up1, lasts = {}, {}
+    for h in (0, 1):
+        for d in (1, 2, 3):
+            up2[h, d].wait_recv()
+        place = out.at[core, h, own[h]]
+        for d in (2, 1, 3):
+            up1[h, d] = send(place, place, up1_s.at[h, d - 1], up1_r.at[h, d - 1], peer(h, d))
+            up1[h, d].start()
+        lasts[h, 0] = send(place, place, last_s.at[h, 0], last_r.at[h, 0], partner)
+        lasts[h, 0].start()
+    for d in (1, 3, 2):
+        for h in (0, 1):
+            up1[h, d].wait_recv()
+            place = out.at[core, h, (own[h] + SIDE - d) % SIDE]
+            lasts[h, d] = send(place, place, last_s.at[h, d], last_r.at[h, d], partner)
+            lasts[h, d].start()
+    for group in (pairs, firsts, seconds, deeps, backs, up2, up1, lasts):
+        for copy in group.values():
+            copy.wait_send()
+    for copy in lasts.values():
+        copy.wait_recv()
+
+
+def reduce_kernels(second_term, first_term, scale):
+    part = jnp.stack([second_term, first_term]).astype(jnp.bfloat16).reshape(2, 2, SIDE, ROWS, 128)
+    part = jnp.pad(part, ((0, 0), (0, 0), (0, 0), (0, PADDED - ROWS), (0, 0)))
+    bf16 = jnp.bfloat16
+    dma = pltpu.SemaphoreType.DMA
+    shapes = [(2, 4), (2, 4), (2, 3), (2, 3), (2, 3), (2, 3), (15,), (15,), (15,), (15,), (2, 3), (2, 3), (2, 3), (2, 3), (2, 4), (2, 4)]
+
+    def kernel(part, out, pair, summed, first_in, second_out, second_in, tiles, deep_in, final, *sems):
+        reduce_body(scale, part, out, pair, summed, first_in, second_out, second_in, tiles, deep_in, final, sems)
+
+    out = pl.pallas_call(
+        kernel,
+        out_shape=jax.ShapeDtypeStruct(part.shape, bf16),
+        in_specs=[pl.BlockSpec(memory_space=pltpu.VMEM)],
+        out_specs=pl.BlockSpec(memory_space=pltpu.VMEM),
+        scratch_shapes=[
+            pltpu.VMEM((2, SIDE, PADDED, 128), bf16),
+            pltpu.VMEM((2, SIDE, PADDED, 128), bf16),
+            pltpu.VMEM((2, 3, PADDED, 128), bf16),
+            pltpu.VMEM((2, SIDE, PIECE, 128), bf16),
+            pltpu.VMEM((2, 3, PIECE, 128), bf16),
+            pltpu.VMEM((DEPTH, TILE, 128), bf16),
+            pltpu.VMEM((DEPTH - 1, TILE, 128), bf16),
+            pltpu.VMEM((DEPTH, TILE, 128), bf16),
+        ] + [dma(s) for s in shapes],
+        compiler_params=pltpu.CompilerParams(collective_id=0, has_side_effects=True),
+        name="reduce_kernels",
+    )(part)
+    out = out[:, :, :, :ROWS].reshape(2, 27, 128, 128)
+    return out[0], out[1]
 
 
 def per_device(inputs, pre_first, occupancy, grad_out, w_first, w_second):
     size_x, size_y, size_z, chans = inputs.shape
     cells_all = size_x * lax.axis_size("brick") * size_y * size_z * lax.axis_size("slab")
-    scale = 10.0 / jnp.sqrt(jnp.float32(cells_all))
+    scale = 10.0 / cells_all**0.5
     occ = occupancy.astype(jnp.float32)[..., None]
     pre = pre_first.astype(jnp.float32)
     sig = jax.nn.sigmoid(pre)
@@ -67,14 +219,13 @@
     cols_second = columns(grad_second_pre)
     grad_act = jnp.dot(cols_second, stacked_kernel(w_second), preferred_element_type=jnp.float32)
     grad_act = grad_act.reshape(inputs.shape)
-    second_term = local_term(act, cols_second, scale)
-    grad_second = reduce_kernel(second_term)
+    second_term = local_term(act, cols_second)
     grad_first_pre = (grad_act * occ * sig * (1.0 + pre * (1.0 - sig))).astype(jnp.bfloat16)
     cols_first = columns(grad_first_pre)
     back = jnp.dot(cols_first, stacked_kernel(w_first), preferred_element_type=jnp.float32)
     grad_in = (grad_out.astype(jnp.float32) + back.reshape(inputs.shape)).astype(jnp.bfloat16)
-    first_term = local_term(inputs, cols_first, scale)
-    grad_first = reduce_kernel(first_term)
+    first_term = local_term(inputs, cols_first)
+    grad_second, grad_first = reduce_kernels(second_term, first_term, scale)
     return (grad_in, grad_first, grad_second)
 
 

time: 283 us -> 154 us (0.54)
  blocking collectives: 193 us -> 0 us
  Pallas kernels: 0 us -> 63.5 us
    psum x1 -> x0, blocking collectives: 193 us -> none  [reduce_kernel(): return lax.psum(term, ('slab', 'brick')).astype(jnp.bfloat16)]
    pallas_call x0 -> x1, Pallas kernels: none -> 63.5 us  [reduce_kernels(): pl.pallas_call(kernel, out_shape=jax.ShapeDtypeStruct(part.shape, bf16),...]
  transfers between devices with their start and end apart: 8 -> 8, of which waited for: 2 -> 2; matrix products, arithmetic and copies ran while one was open for 5% -> 8% of each run, Pallas kernels for 0% -> 0%
where the time goes in v1:
time: 154 us
  Pallas kernels  63.5 us (41%)
  starting transfers between devices  58.4 us (38%)
  local copies, waits for them, and re-layouts  17.5 us (11%)
  matrix products  7.1 us (5%)
  other arithmetic  4.59 us (3%)
  waiting for transfers between devices  1.61 us (1%)
    pallas_call x1, Pallas kernels, reduce_kernels(): pl.pallas_call(kernel, out_shape=jax.ShapeDtypeStruct(part.shape, bf16),...  63.5 us
    ppermute x4, starting transfers between devices, with_halo(): after = lax.ppermute(initial, axis, down)  45.6 us
    ppermute x4, starting transfers between devices, with_halo(): before = lax.ppermute(last, axis, up)  12.8 us
    unnamed x60, local copies, waits for them, and re-layouts  7.52 us
    dot_general x1, local copies, waits for them, and re-layouts, local_term(): lax.dot_general(flat_left, cols, (((0,), (0,)), ((), ())), preferred_elem...  5.76 us
    dot_general x2, matrix products, local_term(): lax.dot_general(flat_left, cols, (((0,), (0,)), ((), ())), preferred_elem...  4.25 us
  transfers between devices with their start and end apart: 8, of which 2 were waited for; matrix products, arithmetic and copies ran while one was open for 8% of the time, Pallas kernels for 0%

profile of v1, /device:TPU:1, one launch (start us, length us, event | category | flops | bytes accessed | tf_op | source)
XLA Modules:
  0.0 153.9 jit_solution(7789556070348005080)
XLA Ops:
  0.6 0.8 convert_element_type.27
  1.4 1.1 fusion.18
  2.6 4.0 %collective-permute-start = (bf16[4,8,1,128]{3,2,1,0:T(2,128)(2,1)S(1)}, bf16[4,8,1,128]{3,2,1,0:T(2,128)(2,1)S(1)}, u32[]{:S(2)}, u32[]{:S(2)}) collective-permute-start(bf16[4,8,1,128]{3,2,1,0:T(2,128)(2,1)S(1)} %get-tuple-element.15), channel_id=1, source_target_pairs={{0,64},{64,128},{128,192},{192,256},{256,320},{320,384},{384,448},... | collective-permute-start | bytes 24584 | tf_op jit(solution)/shard_map/ppermute | solution.py:16
  6.6 16.6 %collective-permute-start.1 = (bf16[4,8,1,128]{3,2,1,0:T(2,128)(2,1)S(1)}, bf16[4,8,1,128]{3,2,1,0:T(2,128)(2,1)S(1)}, u32[]{:S(2)}, u32[]{:S(2)}) collective-permute-start(bf16[4,8,1,128]{3,2,1,0:T(2,128)(2,1)S(1)} %get-tuple-element.16), channel_id=1, source_target_pairs={{64,0},{128,64},{192,128},{256,192},{320,256},{384,320},{448,384},... | collective-permute-start | bytes 24584 | tf_op jit(solution)/shard_map/ppermute | solution.py:17
  23.2 0.8 collective-permute-done.1
  24.1 4.5 %collective-permute-start.2 = (bf16[1,8,18,128]{3,2,1,0:T(8,128)(2,1)S(1)}, bf16[1,8,18,128]{3,2,1,0:T(8,128)(2,1)S(1)}, u32[]{:S(2)}, u32[]{:S(2)}) collective-permute-start(bf16[1,8,18,128]{3,2,1,0:T(8,128)(2,1)S(1)} %get-tuple-element.11), channel_id=1, source_target_pairs={{0,1},{1,2},{2,3},{3,4},{4,5},{5,6},{6,7},{7,8},{8,9},{9,10},{10,1... | collective-permute-start | bytes 110600 | tf_op jit(solution)/shard_map/ppermute | solution.py:16
  28.6 2.7 %collective-permute-start.3 = (bf16[1,8,18,128]{3,2,1,0:T(8,128)(2,1)S(1)}, bf16[1,8,18,128]{3,2,1,0:T(8,128)(2,1)S(1)}, u32[]{:S(2)}, u32[]{:S(2)}) collective-permute-start(bf16[1,8,18,128]{3,2,1,0:T(8,128)(2,1)S(1)} %get-tuple-element.12), channel_id=1, source_target_pairs={{1,0},{2,1},{3,2},{4,3},{5,4},{6,5},{7,6},{8,7},{9,8},{10,9},{11,1... | collective-permute-start | bytes 110600 | tf_op jit(solution)/shard_map/ppermute | solution.py:17
  31.4 1.9 %copy.12 = bf16[27,128,128]{1,2,0:T(8,128)(2,1)S(1)} copy(bf16[27,128,128]{2,1,0:T(8,128)(2,1)} %param.11) | data formatting | bytes 1769472 | tf_op args[5]
  33.3 0.8 collective-permute-done.3
  36.1 1.7 %copy-done.1 = bf16[4,8,16,3456]{3,2,1,0:T(8,128)(2,1)} copy-done((bf16[4,8,16,3456]{3,2,1,0:T(8,128)(2,1)}, bf16[4,8,16,3456]{3,2,1,0:T(8,128)(2,1)S(1)}, u32[]{:S(2)}) %copy-start.1) | copy-done | bytes 3538968
  37.9 1.1 fusion.6
  39.0 1.9 %collective-permute-start.4 = (bf16[4,8,1,128]{3,2,1,0:T(2,128)(2,1)S(1)}, bf16[4,8,1,128]{3,2,1,0:T(2,128)(2,1)S(1)}, u32[]{:S(2)}, u32[]{:S(2)}) collective-permute-start(bf16[4,8,1,128]{3,2,1,0:T(2,128)(2,1)S(1)} %get-tuple-element.13), channel_id=1, source_target_pairs={{0,64},{64,128},{128,192},{192,256},{256,320},{320,384},{384,448},... | collective-permute-start | bytes 24584 | tf_op jit(solution)/shard_map/ppermute | solution.py:16
  41.0 14.7 %collective-permute-start.5 = (bf16[4,8,1,128]{3,2,1,0:T(2,128)(2,1)S(1)}, bf16[4,8,1,128]{3,2,1,0:T(2,128)(2,1)S(1)}, u32[]{:S(2)}, u32[]{:S(2)}) collective-permute-start(bf16[4,8,1,128]{3,2,1,0:T(2,128)(2,1)S(1)} %get-tuple-element.14), channel_id=1, source_target_pairs={{64,0},{128,64},{192,128},{256,192},{320,256},{384,320},{448,384},... | collective-permute-start | bytes 24584 | tf_op jit(solution)/shard_map/ppermute | solution.py:17
  55.7 1.3 copy.13
  57.1 5.8 %copy.14 = bf16[3456,512]{1,0:T(8,128)(2,1)} copy(bf16[3456,512]{0,1:T(8,128)(2,1)} %bitcast.47) | data formatting | bytes 7077888 | tf_op jit(solution)/shard_map/dot_general | solution.py:49
  62.9 2.4 %collective-permute-start.6 = (bf16[1,8,18,128]{3,2,1,0:T(8,128)(2,1)S(1)}, bf16[1,8,18,128]{3,2,1,0:T(8,128)(2,1)S(1)}, u32[]{:S(2)}, u32[]{:S(2)}) collective-permute-start(bf16[1,8,18,128]{3,2,1,0:T(8,128)(2,1)S(1)} %get-tuple-element.7), channel_id=1, source_target_pairs={{0,1},{1,2},{2,3},{3,4},{4,5},{5,6},{6,7},{7,8},{8,9},{9,10},{10,1... | collective-permute-start | bytes 110600 | tf_op jit(solution)/shard_map/ppermute | solution.py:16
  65.2 11.5 %collective-permute-start.7 = (bf16[1,8,18,128]{3,2,1,0:T(8,128)(2,1)S(1)}, bf16[1,8,18,128]{3,2,1,0:T(8,128)(2,1)S(1)}, u32[]{:S(2)}, u32[]{:S(2)}) collective-permute-start(bf16[1,8,18,128]{3,2,1,0:T(8,128)(2,1)S(1)} %get-tuple-element.8), channel_id=1, source_target_pairs={{1,0},{2,1},{3,2},{4,3},{5,4},{6,5},{7,6},{8,7},{9,8},{10,9},{11,1... | collective-permute-start | bytes 110600 | tf_op jit(solution)/shard_map/ppermute | solution.py:17
  76.7 3.1 %convolution_convert_fusion = bf16[128,27,128]{2,0,1:T(8,128)(2,1)S(1)} fusion(bf16[512,128,1]{1,0,2:T(8,128)(2,1)S(1)} %bitcast.55, bf16[27,128,512]{2,1,0:T(8,128)(2,1)} %bitcast.46), kind=kOutput, calls=%fused_computation.6 | convolution fusion | flops 453427200 | bytes 4554752 | tf_op jit(solution)/shard_map/dot_general | solution.py:49
  81.9 1.8 %fusion.7 = bf16[4,8,16,128]{3,2,1,0:T(8,128)(2,1)} fusion(bf16[4,8,16,3456]{3,2,1,0:T(8,128)(2,1)S(1)} %slice_dynamic-update-slice_fusion, bf16[3456,128,1,1]{1,0,3,2:T(8,128)(2,1)S(1)} %bitcast.52, bf16[4,8,16,128]{3,2,1,0:T(8,128)(2,1)S(1)} %copy-done.4), kind=kOutput, calls=%fused_computation.12 | convolution fusion | flops 453181440 | bytes 4685824 | tf_op jit(solution)/shard_map/dot_general | solution.py:225
  83.7 1.1 fusion
  84.8 1.3 copy.16
  86.2 1.5 fusion.3.part
  87.6 63.5 %reduce_kernels.1 = bf16[2,2,4,448,128]{4,3,2,1,0:T(8,128)(2,1)} custom-call(bf16[2,2,4,448,128]{4,3,2,1,0:T(8,128)(2,1)} %fusion.3.part), custom_call_target="tpu_custom_call" | custom-call | tf_op jit(solution)/shard_map/reduce_kernels/pallas_call | solution.py:188
  151.1 2.8 %fusion.23 = (bf16[1,2,4,432,128]{4,3,2,1,0:T(8,128)(2,1)}, bf16[1,2,4,432,128]{4,3,2,1,0:T(8,128)(2,1)}) fusion(bf16[2,2,4,448,128]{4,3,2,1,0:T(8,128)(2,1)} %reduce_kernels.1), kind=kLoop, calls=%fused_computation.112 | loop fusion | bytes 3538944 | tf_op jit(solution)/shard_map/slice | solution.py:207
  (79 shorter events, 4.0 us)
Async XLA Ops:
  0.6 83.1 %copy-start = (bf16[4,8,16,128]{3,2,1,0:T(8,128)(2,1)S(1)}, bf16[4,8,16,128]{3,2,1,0:T(8,128)(2,1)}, u32[]{:S(2)}) copy-start(bf16[4,8,16,128]{3,2,1,0:T(8,128)(2,1)} %param.6) | copy-start | bytes 393220
  2.6 20.6 %collective-permute-start = (bf16[4,8,1,128]{3,2,1,0:T(2,128)(2,1)S(1)}, bf16[4,8,1,128]{3,2,1,0:T(2,128)(2,1)S(1)}, u32[]{:S(2)}, u32[]{:S(2)}) collective-permute-start(bf16[4,8,1,128]{3,2,1,0:T(2,128)(2,1)S(1)} %get-tuple-element.15), channel_id=1, source_target_pairs={{0,64},{64,128},{128,192},{192,256},{256,320},{320,384},{384,448},... | collective-permute-start | bytes 24584 | tf_op jit(solution)/shard_map/ppermute | solution.py:16
  6.6 17.5 %collective-permute-start.1 = (bf16[4,8,1,128]{3,2,1,0:T(2,128)(2,1)S(1)}, bf16[4,8,1,128]{3,2,1,0:T(2,128)(2,1)S(1)}, u32[]{:S(2)}, u32[]{:S(2)}) collective-permute-start(bf16[4,8,1,128]{3,2,1,0:T(2,128)(2,1)S(1)} %get-tuple-element.16), channel_id=1, source_target_pairs={{64,0},{128,64},{192,128},{256,192},{320,256},{384,320},{448,384},... | collective-permute-start | bytes 24584 | tf_op jit(solution)/shard_map/ppermute | solution.py:17
  24.1 9.2 %collective-permute-start.2 = (bf16[1,8,18,128]{3,2,1,0:T(8,128)(2,1)S(1)}, bf16[1,8,18,128]{3,2,1,0:T(8,128)(2,1)S(1)}, u32[]{:S(2)}, u32[]{:S(2)}) collective-permute-start(bf16[1,8,18,128]{3,2,1,0:T(8,128)(2,1)S(1)} %get-tuple-element.11), channel_id=1, source_target_pairs={{0,1},{1,2},{2,3},{3,4},{4,5},{5,6},{6,7},{7,8},{8,9},{9,10},{10,1... | collective-permute-start | bytes 110600 | tf_op jit(solution)/shard_map/ppermute | solution.py:16
  28.6 5.4 %collective-permute-start.3 = (bf16[1,8,18,128]{3,2,1,0:T(8,128)(2,1)S(1)}, bf16[1,8,18,128]{3,2,1,0:T(8,128)(2,1)S(1)}, u32[]{:S(2)}, u32[]{:S(2)}) collective-permute-start(bf16[1,8,18,128]{3,2,1,0:T(8,128)(2,1)S(1)} %get-tuple-element.12), channel_id=1, source_target_pairs={{1,0},{2,1},{3,2},{4,3},{5,4},{6,5},{7,6},{8,7},{9,8},{10,9},{11,1... | collective-permute-start | bytes 110600 | tf_op jit(solution)/shard_map/ppermute | solution.py:17
  34.5 3.4 %copy-start.3 = (bf16[4,8,16,128]{3,2,1,0:T(8,128)(2,1)S(1)}, bf16[4,8,16,128]{3,2,1,0:T(8,128)(2,1)}, u32[]{:S(2)}) copy-start(bf16[4,8,16,128]{3,2,1,0:T(8,128)(2,1)} %param.7) | copy-start | bytes 393220
  35.9 19.8 %copy-start.2 = (bf16[27,128,128]{2,1,0:T(8,128)(2,1)S(1)}, bf16[27,128,128]{2,1,0:T(8,128)(2,1)}, u32[]{:S(2)}) copy-start(bf16[27,128,128]{2,1,0:T(8,128)(2,1)} %param.10) | copy-start | bytes 2654212
  36.1 1.8 %copy-start.1 = (bf16[4,8,16,3456]{3,2,1,0:T(8,128)(2,1)}, bf16[4,8,16,3456]{3,2,1,0:T(8,128)(2,1)S(1)}, u32[]{:S(2)}) copy-start(bf16[4,8,16,3456]{3,2,1,0:T(8,128)(2,1)S(1)} %slice_dynamic-update-slice_fusion.24) | copy-start | bytes 10616836
  39.0 23.8 %collective-permute-start.4 = (bf16[4,8,1,128]{3,2,1,0:T(2,128)(2,1)S(1)}, bf16[4,8,1,128]{3,2,1,0:T(2,128)(2,1)S(1)}, u32[]{:S(2)}, u32[]{:S(2)}) collective-permute-start(bf16[4,8,1,128]{3,2,1,0:T(2,128)(2,1)S(1)} %get-tuple-element.13), channel_id=1, source_target_pairs={{0,64},{64,128},{128,192},{192,256},{256,320},{320,384},{384,448},... | collective-permute-start | bytes 24584 | tf_op jit(solution)/shard_map/ppermute | solution.py:16
  41.0 21.9 %collective-permute-start.5 = (bf16[4,8,1,128]{3,2,1,0:T(2,128)(2,1)S(1)}, bf16[4,8,1,128]{3,2,1,0:T(2,128)(2,1)S(1)}, u32[]{:S(2)}, u32[]{:S(2)}) collective-permute-start(bf16[4,8,1,128]{3,2,1,0:T(2,128)(2,1)S(1)} %get-tuple-element.14), channel_id=1, source_target_pairs={{64,0},{128,64},{192,128},{256,192},{320,256},{384,320},{448,384},... | collective-permute-start | bytes 24584 | tf_op jit(solution)/shard_map/ppermute | solution.py:17
  62.9 17.0 %collective-permute-start.6 = (bf16[1,8,18,128]{3,2,1,0:T(8,128)(2,1)S(1)}, bf16[1,8,18,128]{3,2,1,0:T(8,128)(2,1)S(1)}, u32[]{:S(2)}, u32[]{:S(2)}) collective-permute-start(bf16[1,8,18,128]{3,2,1,0:T(8,128)(2,1)S(1)} %get-tuple-element.7), channel_id=1, source_target_pairs={{0,1},{1,2},{2,3},{3,4},{4,5},{5,6},{6,7},{7,8},{8,9},{9,10},{10,1... | collective-permute-start | bytes 110600 | tf_op jit(solution)/shard_map/ppermute | solution.py:16
  65.2 14.6 %collective-permute-start.7 = (bf16[1,8,18,128]{3,2,1,0:T(8,128)(2,1)S(1)}, bf16[1,8,18,128]{3,2,1,0:T(8,128)(2,1)S(1)}, u32[]{:S(2)}, u32[]{:S(2)}) collective-permute-start(bf16[1,8,18,128]{3,2,1,0:T(8,128)(2,1)S(1)} %get-tuple-element.8), channel_id=1, source_target_pairs={{1,0},{2,1},{3,2},{4,3},{5,4},{6,5},{7,6},{8,7},{9,8},{10,9},{11,1... | collective-permute-start | bytes 110600 | tf_op jit(solution)/shard_map/ppermute | solution.py:17
  80.3 1.6 %copy-start.4 = (bf16[4,8,16,128]{3,2,1,0:T(8,128)(2,1)S(1)}, bf16[4,8,16,128]{3,2,1,0:T(8,128)(2,1)}, u32[]{:S(2)}) copy-start(bf16[4,8,16,128]{3,2,1,0:T(8,128)(2,1)} %param.9) | copy-start | bytes 393220

commit v2 on v1

v2 whole, which is shorter than its diff:
```python
import jax
import jax.numpy as jnp
from jax import lax
from jax.experimental import pallas as pl
from jax.experimental.pallas import tpu as pltpu
from jax.sharding import PartitionSpec as P

ROWS, PADDED, PIECE, TILE, SIDE, DEPTH = 432, 448, 112, 16, 4, 16
F32, BF16 = jnp.float32, jnp.bfloat16
NEAR = [(0, 1), (0, -1), (1, 0), (-1, 0), (1, 1), (1, -1), (-1, 1), (-1, -1)]


def coordinates():
    slab, brick = lax.axis_index("slab"), lax.axis_index("brick")
    return (brick // 2) % 4, slab % 4, (slab // 4) * 8 + brick // 8, brick % 2


def device(x, y, z, core):
    return ((z // 8) * 4 + y, (z % 8) * 8 + x * 2 + core)


def neighbour(ds, db):
    slab, brick = lax.axis_index("slab"), lax.axis_index("brick")
    return ((slab + ds + 8) % 8, (brick + db + 64) % 64)


def send(src, dst, s, r, to):
    return pltpu.make_async_remote_copy(
        src_ref=src, dst_ref=dst, send_sem=s, recv_sem=r, device_id=to,
        device_id_type=pl.DeviceIdType.MESH,
    )


def exchange(own, base, face, zin, s, r):
    copies = []
    for n, (ds, db) in enumerate(NEAR):
        if ds == 0:
            src, dst = own(3 if db == 1 else 0), base.at[0 if db == 1 else 5]
        else:
            side = 0 if ds == 1 else 1
            if db == 0:
                src, dst = face.at[side], zin.at[side, pl.ds(1, 4)]
            else:
                src, dst = face.at[side, 3 if db == 1 else 0], zin.at[side, 0 if db == 1 else 5]
        copies.append(send(src, dst, s.at[n], r.at[n], neighbour(ds, db)))
    order = (2, 3, 4, 5, 6, 7, 0, 1)
    for n in order:
        copies[n].start()
    return copies


def shifted_copies(base, zin, ext):
    def step(i, carry):
        v = base[i]
        wide = v.astype(F32)
        row = lax.broadcasted_iota(jnp.int32, wide.shape, 1)
        before = jnp.broadcast_to(zin[0, i].astype(F32)[:, None, :], wide.shape)
        after = jnp.broadcast_to(zin[1, i].astype(F32)[:, None, :], wide.shape)
        low = jnp.where(row == 15, after, pltpu.roll(wide, 15, 1)).astype(BF16)
        high = jnp.where(row == 0, before, pltpu.roll(wide, 1, 1)).astype(BF16)
        for c, w in enumerate((low, v, high)):
            ext[c, i, pl.ds(1, 8)] = w
            ext[c, i, 0] = w[7]
            ext[c, i, 9] = w[0]
        return carry

    lax.fori_loop(0, 6, step, 0)


def triple(ext, a, b, order):
    parts = [ext[1 + c, pl.ds(1 - a, 4), pl.ds(1 - b, 8)].reshape(512, 128) for c in order]
    return jnp.concatenate(parts, axis=1)


def transpose_conv(ext, w):
    total = None
    for a in (-1, 0, 1):
        for b in (-1, 0, 1):
            k = 9 * (a + 1) + 3 * (b + 1)
            right = jnp.concatenate([w[k], w[k + 1], w[k + 2]], axis=1)
            term = lax.dot_general(triple(ext, a, b, (-1, 0, 1)), right, (((1,), (1,)), ((), ())), preferred_element_type=F32)
            total = term if total is None else total + term
    return total


def put(part, g, k, value):
    value = value.astype(BF16)
    for j in range(8):
        lo, hi = max(128 * k, ROWS * j), min(128 * k + 128, ROWS * j + ROWS)
        if lo < hi:
            part[g, j // 4, j % 4, lo - ROWS * j : hi - ROWS * j] = value[lo - 128 * k : hi - 128 * k]


def body(scale, inputs, gsp, act, slope, grad_out, faces, w1_hbm, w2_hbm, grad_in, out, w1, w2, bases, facebuf, zins, ext, part, pair, summed, first_in, second_out, second_in, tiles, deep_in, final, w_sem, halo_s, halo_r, sems):
    x, y, z, core = coordinates()
    pair_s, pair_r, first_s, first_r, second_s, second_r, deep_s, deep_r, back_s, back_r = sems[:10]
    up2_s, up2_r, up1_s, up1_r, last_s, last_r = sems[10:]
    partner = device(x, y, z, 1 - core)
    own = (x, y)

    def peer(axis, d):
        if axis == 0:
            return device((x + d) % SIDE, y, z, core)
        return device(x, (y + d) % SIDE, z, core)

    def deep(d):
        return device(x, y, (z + d) % DEPTH, core)

    barrier = pltpu.get_barrier_semaphore()
    everyone = [neighbour(ds, db) for ds, db in reversed(NEAR)] + [deep(d) for d in range(1, DEPTH)]
    everyone += [peer(h, d) for h in (0, 1) for d in (1, 2, 3)] + [partner]
    for to in everyone:
        pl.semaphore_signal(barrier, inc=1, device_id=to, device_id_type=pl.DeviceIdType.MESH)
    loads = [pltpu.make_async_copy(w2_hbm, w2, w_sem.at[0]), pltpu.make_async_copy(w1_hbm, w1, w_sem.at[1])]
    for load in loads:
        load.start()
    bases[0, pl.ds(1, 4)] = gsp[...]
    bases[1, pl.ds(1, 4)] = inputs[...]
    for g in (0, 1):
        for c in (0, 1):
            for i in range(SIDE):
                part[g, c, i, ROWS:] = jnp.zeros((PADDED - ROWS, 128), BF16)
    tiles[14:16] = jnp.zeros((2, TILE, 128), BF16)
    act_t = act[...].reshape(512, 128).T
    pl.semaphore_wait(barrier, len(everyone))

    halos = [None, None, None]
    for f, ref in ((0, gsp), (1, inputs)):
        halos[f] = exchange(lambda i, ref=ref: ref.at[i], bases.at[f], faces.at[f], zins.at[f], halo_s.at[f], halo_r.at[f])
    for copy in halos[0]:
        copy.wait_recv()
    shifted_copies(bases.at[0], zins.at[0], ext.at[0])

    pairs = {}
    order = (2, 1, 3, 0)

    def start_pairs(h):
        for d in order:
            slot = (own[h] + d) % SIDE
            pairs[h, d] = send(part.at[h, 1 - core, slot], pair.at[h, slot], pair_s.at[h, d], pair_r.at[h, d], partner)
            pairs[h, d].start()

    for a in (-1, 0, 1):
        for b in (-1, 0, 1):
            k = 9 * (a + 1) + 3 * (b + 1)
            term = jnp.dot(act_t, triple(ext.at[0], a, b, (-1, 0, 1)), preferred_element_type=F32)
            for c in range(3):
                put(part, 0, k + c, term[:, 128 * c : 128 * c + 128])
    start_pairs(0)
    loads[0].wait()
    grad_act = transpose_conv(ext.at[0], w2)
    grad_pre = (grad_act.reshape(4, 8, 16, 128) * slope[...]).astype(BF16)
    bases[2, pl.ds(1, 4)] = grad_pre
    wide = grad_pre.astype(F32)
    facebuf[0] = wide[:, :, 15, :].astype(BF16)
    facebuf[1] = wide[:, :, 0, :].astype(BF16)
    halos[2] = exchange(lambda i: bases.at[2, i + 1], bases.at[2], facebuf, zins.at[2], halo_s.at[2], halo_r.at[2])
    firsts = {}

    def start_firsts(h):
        for d in order:
            slot = (own[h] + d) % SIDE
            pairs[h, d].wait_recv()
            total = part[h, core, slot].astype(F32) + pair[h, slot].astype(F32)
            summed[h, slot] = total.astype(BF16)
            if d:
                firsts[h, d] = send(summed.at[h, slot], first_in.at[h, d - 1], first_s.at[h, d - 1], first_r.at[h, d - 1], peer(h, d))
                firsts[h, d].start()

    start_firsts(0)
    for copy in halos[1]:
        copy.wait_recv()
    shifted_copies(bases.at[1], zins.at[1], ext.at[1])
    grad_t = grad_pre.reshape(512, 128).T
    for a in (-1, 0, 1):
        for b in (-1, 0, 1):
            k = 9 * (a + 1) + 3 * (b + 1)
            term = jnp.dot(grad_t, triple(ext.at[1], -a, -b, (1, 0, -1)), preferred_element_type=F32)
            for c in range(3):
                put(part, 1, k + c, term[:, 128 * c : 128 * c + 128].T)
    start_pairs(1)
    start_firsts(1)
    seconds = {}
    for h in (0, 1):
        for d in (1, 2, 3):
            firsts[h, d].wait_recv()
        total = summed[h, own[h]].astype(F32)
        for d in (1, 2, 3):
            total = total + first_in[h, d - 1].astype(F32)
        second_out[h] = total.astype(BF16).reshape(SIDE, PIECE, 128)
        for d in (2, 1, 3):
            slot = (own[1 - h] + d) % SIDE
            seconds[h, d] = send(second_out.at[h, slot], second_in.at[h, d - 1], second_s.at[h, d - 1], second_r.at[h, d - 1], peer(1 - h, d))
            seconds[h, d].start()
    for h in (0, 1):
        for d in (1, 2, 3):
            seconds[h, d].wait_recv()
        total = second_out[h, own[1 - h]].astype(F32)
        for d in (1, 2, 3):
            total = total + second_in[h, d - 1].astype(F32)
        tiles[7 * h : 7 * h + 7] = total.astype(BF16).reshape(7, TILE, 128)
    far = sorted(range(1, DEPTH), key=lambda d: -min(d, DEPTH - d))
    deeps = {}
    for d in far:
        deeps[d] = send(tiles.at[(z + d) % DEPTH], deep_in.at[d - 1], deep_s.at[d - 1], deep_r.at[d - 1], deep(d))
        deeps[d].start()

    for copy in halos[2]:
        copy.wait_recv()
    shifted_copies(bases.at[2], zins.at[2], ext.at[0])
    loads[1].wait()
    back = transpose_conv(ext.at[0], w1)
    grad_in[...] = (grad_out[...].astype(F32) + back.reshape(4, 8, 16, 128)).astype(BF16)

    total = tiles[z].astype(F32)
    for d in reversed(far):
        deeps[d].wait_recv()
        total = total + deep_in[d - 1].astype(F32)
    final[z] = (total * scale).astype(BF16)
    backs = {}
    for d in far:
        backs[d] = send(final.at[z], final.at[z], back_s.at[d - 1], back_r.at[d - 1], deep(d))
        backs[d].start()
    for d in reversed(far):
        backs[d].wait_recv()
    up2 = {}
    for h in (0, 1):
        rows = pl.ds(pl.multiple_of(own[1 - h] * PIECE, PIECE), PIECE)
        out[h, core, own[h], rows] = final[7 * h : 7 * h + 7].reshape(PIECE, 128)
        place = out.at[h, core, own[h], rows]
        for d in (2, 1, 3):
            up2[h, d] = send(place, place, up2_s.at[h, d - 1], up2_r.at[h, d - 1], peer(1 - h, d))
            up2[h, d].start()
    up1, lasts = {}, {}
    for h in (0, 1):
        for d in (1, 2, 3):
            up2[h, d].wait_recv()
        place = out.at[h, core, own[h]]
        for d in (2, 1, 3):
            up1[h, d] = send(place, place, up1_s.at[h, d - 1], up1_r.at[h, d - 1], peer(h, d))
            up1[h, d].start()
        lasts[h, 0] = send(place, place, last_s.at[h, 0], last_r.at[h, 0], partner)
        lasts[h, 0].start()
    for d in (1, 3, 2):
        for h in (0, 1):
            up1[h, d].wait_recv()
            place = out.at[h, core, (own[h] + SIDE - d) % SIDE]
            lasts[h, d] = send(place, place, last_s.at[h, d], last_r.at[h, d], partner)
            lasts[h, d].start()
    for group in (pairs, firsts, seconds, deeps, backs, up2, up1, lasts):
        for copy in group.values():
            copy.wait_send()
    for copies in halos:
        for copy in copies:
            copy.wait_send()
    for copy in lasts.values():
        copy.wait_recv()


def per_device(inputs, pre_first, occupancy, grad_out, w_first, w_second):
    size_x, size_y, size_z, chans = inputs.shape
    cells_all = size_x * lax.axis_size("brick") * size_y * size_z * lax.axis_size("slab")
    scale = 10.0 / cells_all**0.5
    occ = occupancy.astype(F32)[..., None]
    pre = pre_first.astype(F32)
    sig = jax.nn.sigmoid(pre)
    act = (pre * sig * occ).astype(BF16)
    slope = occ * sig * (1.0 + pre * (1.0 - sig))
    gsp = (grad_out.astype(F32) * occ).astype(BF16)
    faces = jnp.stack([jnp.stack([f[:, :, 15], f[:, :, 0]]) for f in (gsp, inputs)])
    dma = pltpu.SemaphoreType.DMA
    shapes = [(2, 4), (2, 4), (2, 3), (2, 3), (2, 3), (2, 3), (15,), (15,), (15,), (15,), (2, 3), (2, 3), (2, 3), (2, 3), (2, 4), (2, 4)]

    def kernel(*refs):
        body(scale, *refs[:28], refs[28:])

    vmem = pl.BlockSpec(memory_space=pltpu.VMEM)
    hbm = pl.BlockSpec(memory_space=pl.ANY)
    grad_in, out = pl.pallas_call(
        kernel,
        out_shape=(
            jax.ShapeDtypeStruct(inputs.shape, BF16),
            jax.ShapeDtypeStruct((2, 2, SIDE, PADDED, 128), BF16),
        ),
        in_specs=[vmem] * 6 + [hbm] * 2,
        out_specs=(vmem, vmem),
        scratch_shapes=[
            pltpu.VMEM((27, 128, 128), BF16),
            pltpu.VMEM((27, 128, 128), BF16),
            pltpu.VMEM((3, 6, 8, 16, 128), BF16),
            pltpu.VMEM((2, 4, 8, 128), BF16),
            pltpu.VMEM((3, 2, 6, 8, 128), BF16),
            pltpu.VMEM((2, 3, 6, 10, 16, 128), BF16),
            pltpu.VMEM((2, 2, SIDE, PADDED, 128), BF16),
            pltpu.VMEM((2, SIDE, PADDED, 128), BF16),
            pltpu.VMEM((2, SIDE, PADDED, 128), BF16),
            pltpu.VMEM((2, 3, PADDED, 128), BF16),
            pltpu.VMEM((2, SIDE, PIECE, 128), BF16),
            pltpu.VMEM((2, 3, PIECE, 128), BF16),
            pltpu.VMEM((DEPTH, TILE, 128), BF16),
            pltpu.VMEM((DEPTH - 1, TILE, 128), BF16),
            pltpu.VMEM((DEPTH, TILE, 128), BF16),
            dma((2,)), dma((3, 8)), dma((3, 8)),
        ] + [dma(s) for s in shapes],
        compiler_params=pltpu.CompilerParams(collective_id=0, has_side_effects=True),
        name="block_backward",
    )(inputs, gsp, act, slope, grad_out, faces, w_first, w_second)
    out = out[:, :, :, :ROWS].reshape(2, 27, 128, 128)
    return (grad_in, out[1], out[0])


def solution(mesh):
    in_specs = (
        P("brick", None, "slab", None),
        P("brick", None, "slab", None),
        P("brick", None, "slab"),
        P("brick", None, "slab", None),
        P(),
        P(),
    )
    out_specs = (P("brick", None, "slab", None), P(), P())
    return jax.shard_map(
        per_device, mesh=mesh, in_specs=in_specs, out_specs=out_specs, check_vma=False
    )
```

time: 154 us -> 83.5 us (0.54)
  starting transfers between devices: 58.4 us -> 0 us
  local copies, waits for them, and re-layouts: 17.5 us -> 6.72 us
  Pallas kernels: 63.5 us -> 73.4 us
  matrix products: 7.1 us -> 0 us
  other arithmetic: 4.59 us -> 2.5 us
  waiting for transfers between devices: 1.61 us -> 0 us
    ppermute x8 -> x0, starting transfers between devices: 58.4 us -> none  [the longest x4 45.6 us: with_halo(): after = lax.ppermute(initial, axis, down)]
    pallas_call x1, Pallas kernels: 63.5 us -> 73.4 us  [per_device(): pl.pallas_call(kernel, out_shape=(jax.ShapeDtypeStruct(inputs.shape, BF16...]
    dot_general x4 -> x0, matrix products: 7.1 us -> none  [the longest x2 4.25 us: local_term(): lax.dot_general(flat_left, cols, (((0,), (0,)), ((), ())), preferred_elem...]
    unnamed x60 -> x3, local copies, waits for them, and re-layouts: 7.52 us -> 0.66 us
    dot_general x1 -> x0, local copies, waits for them, and re-layouts: 5.76 us -> none  [local_term(): lax.dot_general(flat_left, cols, (((0,), (0,)), ((), ())), preferred_elem...]
    ppermute x8 -> x0, waiting for transfers between devices: 1.61 us -> none  [the longest x4 1.6 us: with_halo(): after = lax.ppermute(initial, axis, down)]
    slice x3 -> x2, local copies, waits for them, and re-layouts: 2.82 us -> 3.69 us  [the longest x1 2.79 us: per_device(): return (grad_in, out[1], out[0])]
  transfers between devices with their start and end apart: 8 -> 0, of which waited for: 2 -> 0; matrix products, arithmetic and copies ran while one was open for 8% -> 0% of each run, Pallas kernels for 0% -> 0%
where the time goes in v2:
time: 83.5 us; the launch traced here: 83.2 us
  Pallas kernels  73.4 us (88%)
  local copies, waits for them, and re-layouts  6.72 us (8%)
  other arithmetic  2.5 us (3%)
    pallas_call x1, Pallas kernels, per_device(): pl.pallas_call(kernel, out_shape=(jax.ShapeDtypeStruct(inputs.shape, BF16...  73.4 us
    slice x1, local copies, waits for them, and re-layouts, per_device(): return (grad_in, out[1], out[0])  2.79 us

profile of v2, /device:TPU:1, one launch (start us, length us, event | category | flops | bytes accessed | tf_op | source)
XLA Modules:
  0.0 83.2 jit_solution(16433738979094727306)
XLA Ops:
  0.6 0.7 convert_element_type.16
  1.4 0.1 copy.10
  1.4 0.9 %fusion.8 = (bf16[4,8,1,128]{3,2,1,0:T(2,128)(2,1)S(1)}, bf16[4,8,1,128]{3,2,1,0:T(2,128)(2,1)S(1)}) fusion(bf16[4,8,16,128]{3,2,1,0:T(8,128)(2,1)} %refs_0_.1), kind=kLoop, calls=%fused_computation.19 | loop fusion | bytes 32768 | tf_op jit(solution)/shard_map/slice | solution.py:270
  2.4 1.2 %fusion.6 = (f32[4,8,16,128]{3,1,0,2:T(8,128)S(1)}, bf16[4,8,16,128]{3,1,0,2:T(8,128)(2,1)S(1)}, bf16[4,8,16,128]{3,1,0,2:T(8,128)(2,1)S(1)}) fusion(f32[4,8,16]{1,0,2:T(4,128)S(1)} %copy.10, bf16[4,8,16,128]{3,2,1,0:T(8,128)(2,1)} %param.7, bf16[4,8,16,128]{3,2,1,0:T(8,128)(2,1)} %refs_4_.1), kind=kLoop, calls=%fused_computation.9 | loop fusion | flops 983040 | bytes 788480 | tf_op jit(solution)/shard_map/mul | solution.py:268
  3.5 0.9 %copy.16.refs_3_ = f32[4,8,16,128]{3,2,1,0:T(8,128)} copy(f32[4,8,16,128]{3,1,0,2:T(8,128)S(1)} %get-tuple-element.9) | data formatting | bytes 524288 | tf_op jit(solution)/shard_map/mul | solution.py:268
  4.4 0.7 copy.14.refs_1_
  5.1 0.6 pad_maximum_fusion.refs_5_
  5.7 0.7 copy.15.refs_2_
  6.4 73.4 %block_backward.1 = (bf16[4,8,16,128]{3,2,1,0:T(8,128)(2,1)}, bf16[2,2,4,448,128]{4,3,2,1,0:T(8,128)(2,1)}) custom-call(bf16[4,8,16,128]{3,2,1,0:T(8,128)(2,1)} %refs_0_.1, bf16[4,8,16,128]{3,2,1,0:T(8,128)(2,1)} %copy.14.refs_1_, bf16[4,8,16,128]{3,2,1,0:T(8,128)(2,1)} %copy.15.refs_2_, f32[4,8,16,128]{3,2,1,0:T(8,128)} %copy.16.refs_3_, ...), custom_call_target="tpu_custom_call" | custom-call | tf_op jit(solution)/shard_map/block_backward/pallas_call | solution.py:279
  79.8 0.0 copy-start
  79.8 2.8 %fusion.7 = (bf16[1,2,4,432,128]{4,3,2,1,0:T(8,128)(2,1)}, bf16[1,2,4,432,128]{4,3,2,1,0:T(8,128)(2,1)}) fusion(bf16[2,2,4,448,128]{4,3,2,1,0:T(8,128)(2,1)} %get-tuple-element.6), kind=kLoop, calls=%fused_computation.18 | loop fusion | bytes 3538944 | tf_op jit(solution)/shard_map/slice | solution.py:309
  82.6 0.0 copy-done
  82.6 0.7 copy.25
  (4 shorter events, 0.0 us)
Async XLA Ops:
  79.8 2.8 %copy-start = (bf16[4,8,16,128]{3,2,1,0:T(8,128)(2,1)S(1)}, bf16[4,8,16,128]{3,2,1,0:T(8,128)(2,1)}, u32[]{:S(2)}) copy-start(bf16[4,8,16,128]{3,2,1,0:T(8,128)(2,1)} %get-tuple-element.21) | copy-start | bytes 393220

commit v3 on v2

v3 whole, which is shorter than its diff:
```python
import jax
import jax.numpy as jnp
from jax import lax
from jax.experimental import pallas as pl
from jax.experimental.pallas import tpu as pltpu
from jax.sharding import PartitionSpec as P

ROWS, PADDED, HALF, PIECE, TILE, SIDE, DEPTH = 432, 448, 224, 112, 16, 4, 16
F32, BF16 = jnp.float32, jnp.bfloat16
NEAR = [(0, 1), (0, -1), (1, 0), (-1, 0), (1, 1), (1, -1), (-1, 1), (-1, -1)]


def coordinates():
    slab, brick = lax.axis_index("slab"), lax.axis_index("brick")
    return (brick // 2) % 4, slab % 4, (slab // 4) * 8 + brick // 8, brick % 2


def device(x, y, z, core):
    return ((z // 8) * 4 + y, (z % 8) * 8 + x * 2 + core)


def neighbour(ds, db):
    slab, brick = lax.axis_index("slab"), lax.axis_index("brick")
    return ((slab + ds + 8) % 8, (brick + db + 64) % 64)


def send(src, dst, s, r, to):
    return pltpu.make_async_remote_copy(
        src_ref=src, dst_ref=dst, send_sem=s, recv_sem=r, device_id=to,
        device_id_type=pl.DeviceIdType.MESH,
    )


def exchange(base, face, zin, s, r):
    copies = []
    for n, (ds, db) in enumerate(NEAR):
        if ds == 0:
            src, dst = base.at[4 if db == 1 else 1], base.at[0 if db == 1 else 5]
        else:
            side = 0 if ds == 1 else 1
            if db == 0:
                src, dst = face.at[side], zin.at[side, pl.ds(1, 4)]
            else:
                src, dst = face.at[side, 3 if db == 1 else 0], zin.at[side, 0 if db == 1 else 5]
        copies.append(send(src, dst, s.at[n], r.at[n], neighbour(ds, db)))
    order = (2, 3, 4, 5, 6, 7, 0, 1)
    for n in order:
        copies[n].start()
    return copies


def shifted_copies(base, zin, ext):
    def step(i, carry):
        v = base[i]
        wide = v.astype(F32)
        row = lax.broadcasted_iota(jnp.int32, wide.shape, 1)
        before = jnp.broadcast_to(zin[0, i].astype(F32)[:, None, :], wide.shape)
        after = jnp.broadcast_to(zin[1, i].astype(F32)[:, None, :], wide.shape)
        low = jnp.where(row == 15, after, pltpu.roll(wide, 15, 1)).astype(BF16)
        high = jnp.where(row == 0, before, pltpu.roll(wide, 1, 1)).astype(BF16)
        for c, w in enumerate((low, v, high)):
            ext[c, i, pl.ds(1, 8)] = w
            ext[c, i, 0] = w[7]
            ext[c, i, 9] = w[0]
        return carry

    lax.fori_loop(0, 6, step, 0)


def triple(ext, a, b, order):
    parts = [ext[1 + c, pl.ds(1 - a, 4), pl.ds(1 - b, 8)].reshape(512, 128) for c in order]
    return jnp.concatenate(parts, axis=1)


def transpose_conv(ext, w):
    total = None
    for a in (-1, 0, 1):
        for b in (-1, 0, 1):
            k = 9 * (a + 1) + 3 * (b + 1)
            right = jnp.concatenate([w[k], w[k + 1], w[k + 2]], axis=1)
            term = lax.dot_general(triple(ext, a, b, (-1, 0, 1)), right, (((1,), (1,)), ((), ())), preferred_element_type=F32)
            total = term if total is None else total + term
    return total


def put(part, g, k, value):
    value = value.astype(BF16)
    for j in range(8):
        lo, hi = max(128 * k, ROWS * j), min(128 * k + 128, ROWS * j + ROWS)
        if lo < hi:
            part[g, j % 2, j // 2, lo - ROWS * j : hi - ROWS * j] = value[lo - 128 * k : hi - 128 * k]


def body(scale, inputs_hbm, pre_hbm, occ_hbm, grad_out_hbm, w1_hbm, w2_hbm, grad_in, first_hbm, second_hbm, pre, occ_in, grad_out, act, slope, w1, w2, bases, faces, zins, ext, part, pair, summed, stage, mid, first_in, second_out, second_in, tiles, deep_in, final, out, load_sem, halo_s, halo_r, store_sem, sems):
    x, y, z, core = coordinates()
    pair_s, pair_r, first_s, first_r, second_s, second_r, deep_s, deep_r, back_s, back_r = sems[:10]
    up2_s, up2_r, up1_s, up1_r, last_s, last_r = sems[10:]
    partner = device(x, y, z, 1 - core)
    own = (x, y)

    def peer(axis, d):
        if axis == 0:
            return device((x + d) % SIDE, y, z, core)
        return device(x, (y + d) % SIDE, z, core)

    def deep(d):
        return device(x, y, (z + d) % DEPTH, core)

    barrier = pltpu.get_barrier_semaphore()
    everyone = [neighbour(ds, db) for ds, db in reversed(NEAR)] + [deep(d) for d in range(1, DEPTH)]
    everyone += [peer(h, d) for h in (0, 1) for d in (1, 2, 3)] + [partner]
    for to in everyone:
        pl.semaphore_signal(barrier, inc=1, device_id=to, device_id_type=pl.DeviceIdType.MESH)
    loads = [
        pltpu.make_async_copy(src, dst, load_sem.at[n])
        for n, (src, dst) in enumerate(
            (
                (occ_hbm, occ_in),
                (grad_out_hbm, grad_out),
                (inputs_hbm, bases.at[1, pl.ds(1, 4)]),
                (pre_hbm, pre),
                (w2_hbm, w2),
                (w1_hbm, w1),
            )
        )
    ]
    for load in loads:
        load.start()
    for g in (0, 1):
        for c in (0, 1):
            for i in range(SIDE):
                part[g, c, i, ROWS:] = jnp.zeros((PADDED - ROWS, 128), BF16)
    tiles[14:16] = jnp.zeros((2, TILE, 128), BF16)

    def mask(i):
        row = occ_in[i].astype(F32)
        wide = jnp.broadcast_to(row[:, None, :], (8, 16, 16))
        here = lax.broadcasted_iota(jnp.int32, wide.shape, 1) == lax.broadcasted_iota(jnp.int32, wide.shape, 2)
        return jnp.sum(jnp.where(here, wide, 0.0), axis=2, keepdims=True)

    def set_faces(f, i, value):
        faces[f, 0, i] = value[:, 15, :].astype(BF16)
        faces[f, 1, i] = value[:, 0, :].astype(BF16)

    def masked(i, carry):
        value = grad_out[i].astype(F32) * mask(i)
        bases[0, i + 1] = value.astype(BF16)
        set_faces(0, i, value)
        set_faces(1, i, bases[1, i + 1].astype(F32))
        return carry

    for n in (0, 1, 2):
        loads[n].wait()
    lax.fori_loop(0, 4, masked, 0)
    pl.semaphore_wait(barrier, len(everyone))

    halos = [exchange(bases.at[f], faces.at[f], zins.at[f], halo_s.at[f], halo_r.at[f]) for f in (0, 1)]

    def pointwise(i, carry):
        v, occ = pre[i].astype(F32), mask(i)
        sig = 1.0 / (1.0 + jnp.exp(-v))
        act[i] = (v * sig * occ).astype(BF16)
        slope[i] = occ * sig * (1.0 + v * (1.0 - sig))
        return carry

    loads[3].wait()
    lax.fori_loop(0, 4, pointwise, 0)
    act_t = act[...].reshape(512, 128).T
    loads[4].wait()
    loads[5].wait()
    for copy in halos[0]:
        copy.wait_recv()
    shifted_copies(bases.at[0], zins.at[0], ext.at[0])

    pairs, firsts, seconds = {}, {}, {}

    def pair_copy(h, i):
        return send(part.at[h, 1 - core, i], pair.at[h, i], pair_s.at[h, i], pair_r.at[h, i], partner)

    def start_pairs(h, ab):
        for i in range(SIDE):
            if 384 * ab < 2 * ROWS * (i + 1) <= 384 * (ab + 1):
                pairs[h, i] = pair_copy(h, i)
                pairs[h, i].start()

    def start_firsts(h):
        def add(d):
            slot = (own[h] + d) % SIDE
            pair_copy(h, slot).wait_recv()
            total = part[h, core, slot].astype(F32) + pair[h, slot].astype(F32)
            summed[h, slot] = total.astype(BF16)
            return summed.at[h, slot]

        def go(n, src, dst, d):
            firsts[h, n] = send(src, dst, first_s.at[h, n], first_r.at[h, n], peer(h, d))
            firsts[h, n].start()

        low, high = pl.ds(0, HALF), pl.ds(HALF, HALF)
        ref = add(2)
        go(0, ref.at[low], stage.at[h, 0], 1)
        go(1, ref.at[high], stage.at[h, 1], 3)
        go(2, add(1).at[high], first_in.at[h, 0, high], 1)
        go(3, add(3).at[low], first_in.at[h, 1, low], 3)
        add(0)

    def forward_firsts(h):
        for n, d in ((0, 1), (1, 3)):
            slot = (own[h] + d) % SIDE
            rows = pl.ds(HALF * n, HALF)
            firsts[h, n].wait_recv()
            mid[h, n] = (summed[h, slot, rows].astype(F32) + stage[h, n].astype(F32)).astype(BF16)
            firsts[h, 4 + n] = send(mid.at[h, n], first_in.at[h, n, rows], first_s.at[h, 4 + n], first_r.at[h, 4 + n], peer(h, d))
            firsts[h, 4 + n].start()

    def start_seconds(h):
        for n in (2, 3, 4, 5):
            firsts[h, n].wait_recv()
        total = summed[h, own[h]].astype(F32) + first_in[h, 0].astype(F32) + first_in[h, 1].astype(F32)
        second_out[h] = total.astype(BF16).reshape(SIDE, PIECE, 128)
        for d in (2, 1, 3):
            slot = (own[1 - h] + d) % SIDE
            seconds[h, d] = send(second_out.at[h, slot], second_in.at[h, d - 1], second_s.at[h, d - 1], second_r.at[h, d - 1], peer(1 - h, d))
            seconds[h, d].start()

    for a in (-1, 0, 1):
        for b in (-1, 0, 1):
            k = 9 * (a + 1) + 3 * (b + 1)
            term = jnp.dot(act_t, triple(ext.at[0], a, b, (-1, 0, 1)), preferred_element_type=F32)
            for c in range(3):
                put(part, 0, k + c, term[:, 128 * c : 128 * c + 128])
            start_pairs(0, k // 3)
    grad_act = transpose_conv(ext.at[0], w2)
    grad_pre = (grad_act.reshape(4, 8, 16, 128) * slope[...]).astype(BF16)
    bases[2, pl.ds(1, 4)] = grad_pre
    wide = grad_pre.astype(F32)
    faces[2, 0] = wide[:, :, 15, :].astype(BF16)
    faces[2, 1] = wide[:, :, 0, :].astype(BF16)
    halos.append(exchange(bases.at[2], faces.at[2], zins.at[2], halo_s.at[2], halo_r.at[2]))
    start_firsts(0)
    for copy in halos[1]:
        copy.wait_recv()
    shifted_copies(bases.at[1], zins.at[1], ext.at[1])
    forward_firsts(0)
    grad_t = grad_pre.reshape(512, 128).T
    for a in (-1, 0, 1):
        for b in (-1, 0, 1):
            k = 9 * (a + 1) + 3 * (b + 1)
            term = jnp.dot(grad_t, triple(ext.at[1], -a, -b, (1, 0, -1)), preferred_element_type=F32)
            for c in range(3):
                put(part, 1, k + c, term[:, 128 * c : 128 * c + 128].T)
            start_pairs(1, k // 3)
    start_firsts(1)
    start_seconds(0)
    forward_firsts(1)
    start_seconds(1)
    for h in (0, 1):
        for d in (1, 2, 3):
            seconds[h, d].wait_recv()
        total = second_out[h, own[1 - h]].astype(F32)
        for d in (1, 2, 3):
            total = total + second_in[h, d - 1].astype(F32)
        tiles[7 * h : 7 * h + 7] = total.astype(BF16).reshape(7, TILE, 128)
    far = sorted(range(1, DEPTH), key=lambda d: -min(d, DEPTH - d))
    deeps = {}
    for d in far:
        deeps[d] = send(tiles.at[(z + d) % DEPTH], deep_in.at[d - 1], deep_s.at[d - 1], deep_r.at[d - 1], deep(d))
        deeps[d].start()

    for copy in halos[2]:
        copy.wait_recv()
    shifted_copies(bases.at[2], zins.at[2], ext.at[0])
    back = transpose_conv(ext.at[0], w1)
    grad_in[...] = (grad_out[...].astype(F32) + back.reshape(4, 8, 16, 128)).astype(BF16)

    total = tiles[z].astype(F32)
    for d in reversed(far):
        deeps[d].wait_recv()
        total = total + deep_in[d - 1].astype(F32)
    final[z] = (total * scale).astype(BF16)
    backs = {}
    for d in far:
        backs[d] = send(final.at[z], final.at[z], back_s.at[d - 1], back_r.at[d - 1], deep(d))
        backs[d].start()
    for d in reversed(far):
        backs[d].wait_recv()
    up2 = {}
    for h in (0, 1):
        rows = pl.ds(pl.multiple_of(own[1 - h] * PIECE, PIECE), PIECE)
        out[h, core, own[h], rows] = final[7 * h : 7 * h + 7].reshape(PIECE, 128)
        place = out.at[h, core, own[h], rows]
        for d in (2, 1, 3):
            up2[h, d] = send(place, place, up2_s.at[h, d - 1], up2_r.at[h, d - 1], peer(1 - h, d))
            up2[h, d].start()
    up1, lasts, stores = {}, {}, []

    def store(h, c, slot):
        rows = pl.ds(pl.multiple_of((2 * slot + c) * ROWS, TILE), ROWS)
        result = (second_hbm, first_hbm)[h]
        stores.append(pltpu.make_async_copy(out.at[h, c, slot, pl.ds(0, ROWS)], result.at[rows], store_sem.at[h, c, slot]))
        stores[-1].start()

    def up(h, n, place, d):
        up1[h, n] = send(place, place, up1_s.at[h, n], up1_r.at[h, n], peer(h, d))
        up1[h, n].start()

    def share(h, d):
        slot = (own[h] + d) % SIDE
        lasts[h, d] = send(out.at[h, core, slot], out.at[h, core, slot], last_s.at[h, d], last_r.at[h, d], partner)
        lasts[h, d].start()
        store(h, core, slot)

    for h in (0, 1):
        for d in (1, 2, 3):
            up2[h, d].wait_recv()
        up(h, 0, out.at[h, core, own[h]], 1)
        up(h, 1, out.at[h, core, own[h]], 3)
        share(h, 0)
    for n, came, d in ((0, 3, 1), (1, 1, 3)):
        for h in (0, 1):
            up1[h, n].wait_recv()
            up(h, 2 + n, out.at[h, core, (own[h] + came) % SIDE, pl.ds(HALF * n, HALF)], d)
            share(h, came)
    for d in (0, 3, 1):
        for h in (0, 1):
            lasts[h, d].wait_recv()
            store(h, 1 - core, (own[h] + d) % SIDE)
    for h in (0, 1):
        up1[h, 2].wait_recv()
        up1[h, 3].wait_recv()
        share(h, 2)
    for h in (0, 1):
        lasts[h, 2].wait_recv()
        store(h, 1 - core, (own[h] + 2) % SIDE)
    for group in (pairs, firsts, seconds, deeps, backs, up2, up1, lasts):
        for copy in group.values():
            copy.wait_send()
    for copies in halos:
        for copy in copies:
            copy.wait_send()
    for copy in stores:
        copy.wait()


def per_device(inputs, pre_first, occupancy, grad_out, w_first, w_second):
    size_x, size_y, size_z, chans = inputs.shape
    cells_all = size_x * lax.axis_size("brick") * size_y * size_z * lax.axis_size("slab")
    scale = 10.0 / cells_all**0.5
    dma = pltpu.SemaphoreType.DMA
    shapes = [(2, 4), (2, 4), (2, 6), (2, 6), (2, 3), (2, 3), (15,), (15,), (15,), (15,), (2, 3), (2, 3), (2, 4), (2, 4), (2, 4), (2, 4)]

    def kernel(*refs):
        body(scale, *refs[:36], refs[36:])

    vmem = pl.BlockSpec(memory_space=pltpu.VMEM)
    hbm = pl.BlockSpec(memory_space=pl.ANY)
    grad_in, grad_first, grad_second = pl.pallas_call(
        kernel,
        out_shape=(
            jax.ShapeDtypeStruct(inputs.shape, BF16),
            jax.ShapeDtypeStruct((8 * ROWS, 128), BF16),
            jax.ShapeDtypeStruct((8 * ROWS, 128), BF16),
        ),
        in_specs=[hbm] * 6,
        out_specs=(vmem, hbm, hbm),
        scratch_shapes=[
            pltpu.VMEM((4, 8, 16, 128), BF16),
            pltpu.VMEM((4, 8, 16), jnp.int32),
            pltpu.VMEM((4, 8, 16, 128), BF16),
            pltpu.VMEM((4, 8, 16, 128), BF16),
            pltpu.VMEM((4, 8, 16, 128), F32),
            pltpu.VMEM((27, 128, 128), BF16),
            pltpu.VMEM((27, 128, 128), BF16),
            pltpu.VMEM((3, 6, 8, 16, 128), BF16),
            pltpu.VMEM((3, 2, 4, 8, 128), BF16),
            pltpu.VMEM((3, 2, 6, 8, 128), BF16),
            pltpu.VMEM((2, 3, 6, 10, 16, 128), BF16),
            pltpu.VMEM((2, 2, SIDE, PADDED, 128), BF16),
            pltpu.VMEM((2, SIDE, PADDED, 128), BF16),
            pltpu.VMEM((2, SIDE, PADDED, 128), BF16),
            pltpu.VMEM((2, 2, HALF, 128), BF16),
            pltpu.VMEM((2, 2, HALF, 128), BF16),
            pltpu.VMEM((2, 2, PADDED, 128), BF16),
            pltpu.VMEM((2, SIDE, PIECE, 128), BF16),
            pltpu.VMEM((2, 3, PIECE, 128), BF16),
            pltpu.VMEM((DEPTH, TILE, 128), BF16),
            pltpu.VMEM((DEPTH - 1, TILE, 128), BF16),
            pltpu.VMEM((DEPTH, TILE, 128), BF16),
            pltpu.VMEM((2, 2, SIDE, PADDED, 128), BF16),
            dma((6,)), dma((3, 8)), dma((3, 8)), dma((2, 2, SIDE)),
        ] + [dma(s) for s in shapes],
        compiler_params=pltpu.CompilerParams(collective_id=0, has_side_effects=True),
        name="block_backward",
    )(inputs, pre_first, occupancy, grad_out, w_first, w_second)
    return (grad_in, grad_first.reshape(w_first.shape), grad_second.reshape(w_second.shape))


def solution(mesh):
    in_specs = (
        P("brick", None, "slab", None),
        P("brick", None, "slab", None),
        P("brick", None, "slab"),
        P("brick", None, "slab", None),
        P(),
        P(),
    )
    out_specs = (P("brick", None, "slab", None), P(), P())
    return jax.shard_map(
        per_device, mesh=mesh, in_specs=in_specs, out_specs=out_specs, check_vma=False
    )
```

time: 83.5 us -> 83.1 us (level)
  Pallas kernels: 73.4 us -> 77.6 us
  other arithmetic: 2.5 us -> 0 us
  local copies, waits for them, and re-layouts: 6.72 us -> 4.74 us
    pallas_call x1, Pallas kernels: 73.4 us -> 77.6 us  [per_device(): pl.pallas_call(kernel, out_shape=(jax.ShapeDtypeStruct(inputs.shape, BF16...]
    unnamed x3 -> x5, local copies, waits for them, and re-layouts: 0.66 us -> 4.74 us
    slice x2 -> x0, local copies, waits for them, and re-layouts: 3.69 us -> none  [the longest x1 2.79 us: per_device(): return (grad_in, out[1], out[0])]
    convert_element_type x3 -> x0, local copies, waits for them, and re-layouts: 1.5 us -> none  [the longest x1 0.71 us: per_device(): act = (pre * sig * occ).astype(BF16)]
    mul x1 -> x0, other arithmetic: 1.15 us -> none  [per_device(): slope = occ * sig * (1.0 + pre * (1.0 - sig))]
    mul x1 -> x0, local copies, waits for them, and re-layouts: 0.86 us -> none  [per_device(): slope = occ * sig * (1.0 + pre * (1.0 - sig))]
where the time goes in v3:
time: 83.1 us; the launch traced here: 82.9 us
  Pallas kernels  77.6 us (93%)
  local copies, waits for them, and re-layouts  4.74 us (6%)
    pallas_call x1, Pallas kernels, per_device(): pl.pallas_call(kernel, out_shape=(jax.ShapeDtypeStruct(inputs.shape, BF16...  77.6 us
    unnamed x5, local copies, waits for them, and re-layouts  4.74 us

profile of v3, /device:TPU:1, one launch (start us, length us, event | category | flops | bytes accessed | tf_op | source)
XLA Modules:
  0.0 82.9 jit_solution(8533086400190320983)
XLA Ops:
  0.6 77.6 %block_backward.1 = (bf16[4,8,16,128]{3,2,1,0:T(8,128)(2,1)}, bf16[3456,128]{1,0:T(8,128)(2,1)}, bf16[3456,128]{1,0:T(8,128)(2,1)}) custom-call(bf16[4,8,16,128]{3,2,1,0:T(8,128)(2,1)} %refs_0_.1, bf16[4,8,16,128]{3,2,1,0:T(8,128)(2,1)} %refs_1_.1, s32[4,8,16]{2,1,0:T(8,128)} %refs_2_.1, bf16[4,8,16,128]{3,2,1,0:T(8,128)(2,1)} %refs_3_.1, ...), custom_call_target="tpu_custom_call" | custom-call | tf_op jit(solution)/shard_map/block_backward/pallas_call | solution.py:356
  78.2 1.6 %copy.12 = bf16[4,8,16,128]{3,2,1,0:T(8,128)(2,1)} copy(bf16[4,8,16,128]{3,2,1,0:T(8,128)(2,1)} %get-tuple-element.12) | data formatting | bytes 262144
  79.8 0.0 copy-start
  79.8 2.3 %copy.13 = bf16[27,128,128]{2,1,0:T(8,128)(2,1)} copy(bf16[27,128,128]{2,1,0:T(8,128)(2,1)} %bitcast.3) | data formatting | bytes 1769472
  82.0 0.0 copy-done
  82.0 0.9 %copy.14 = bf16[27,128,128]{2,1,0:T(8,128)(2,1)} copy(bf16[27,128,128]{2,1,0:T(8,128)(2,1)S(1)} %bitcast.2) | data formatting | bytes 1769472
Async XLA Ops:
  79.8 2.3 %copy-start = (bf16[3456,128]{1,0:T(8,128)(2,1)S(1)}, bf16[3456,128]{1,0:T(8,128)(2,1)}, u32[]{:S(2)}) copy-start(bf16[3456,128]{1,0:T(8,128)(2,1)} %get-tuple-element.8) | copy-start | bytes 2654212

commit v4 on v3

--- a/solution.py
+++ b/solution.py
@@ -293,44 +293,68 @@
             up2[h, d].start()
     up1, lasts, stores = {}, {}, []
 
-    def store(h, c, slot):
-        rows = pl.ds(pl.multiple_of((2 * slot + c) * ROWS, TILE), ROWS)
+    halves = (pl.ds(0, HALF), pl.ds(HALF, HALF))
+    lengths = (HALF, ROWS - HALF)
+
+    def store(h, c, slot, n):
+        rows = pl.ds(pl.multiple_of((2 * slot + c) * ROWS + HALF * n, TILE), lengths[n])
         result = (second_hbm, first_hbm)[h]
-        stores.append(pltpu.make_async_copy(out.at[h, c, slot, pl.ds(0, ROWS)], result.at[rows], store_sem.at[h, c, slot]))
+        src = out.at[h, c, slot, pl.ds(HALF * n, lengths[n])]
+        stores.append(pltpu.make_async_copy(src, result.at[rows], store_sem.at[h, c, slot, n]))
         stores[-1].start()
 
-    def up(h, n, place, d):
-        up1[h, n] = send(place, place, up1_s.at[h, n], up1_r.at[h, n], peer(h, d))
-        up1[h, n].start()
-
-    def share(h, d):
-        slot = (own[h] + d) % SIDE
-        lasts[h, d] = send(out.at[h, core, slot], out.at[h, core, slot], last_s.at[h, d], last_r.at[h, d], partner)
-        lasts[h, d].start()
-        store(h, core, slot)
+    def up(h, m, came, n, d):
+        place = out.at[h, core, (own[h] + came) % SIDE, halves[n]]
+        up1[h, m] = send(place, place, up1_s.at[h, m], up1_r.at[h, m], peer(h, d))
+        up1[h, m].start()
+
+    def share(h, came, n):
+        slot = (own[h] + came) % SIDE
+        place = out.at[h, core, slot, halves[n]]
+        lasts[h, came, n] = send(place, place, last_s.at[h, came, n], last_r.at[h, came, n], partner)
+        lasts[h, came, n].start()
+        store(h, core, slot, n)
+
+    def keep(h, came, n):
+        lasts[h, came, n].wait_recv()
+        store(h, 1 - core, (own[h] + came) % SIDE, n)
 
     for h in (0, 1):
         for d in (1, 2, 3):
             up2[h, d].wait_recv()
-        up(h, 0, out.at[h, core, own[h]], 1)
-        up(h, 1, out.at[h, core, own[h]], 3)
-        share(h, 0)
-    for n, came, d in ((0, 3, 1), (1, 1, 3)):
-        for h in (0, 1):
-            up1[h, n].wait_recv()
-            up(h, 2 + n, out.at[h, core, (own[h] + came) % SIDE, pl.ds(HALF * n, HALF)], d)
-            share(h, came)
-    for d in (0, 3, 1):
-        for h in (0, 1):
-            lasts[h, d].wait_recv()
-            store(h, 1 - core, (own[h] + d) % SIDE)
+        up(h, 0, 0, 0, 1)
+        up(h, 1, 0, 1, 3)
+        up(h, 2, 0, 1, 1)
+        up(h, 3, 0, 0, 3)
+        share(h, 0, 0)
+        share(h, 0, 1)
+    for h in (0, 1):
+        up1[h, 0].wait_recv()
+        up(h, 4, 3, 0, 1)
+        up1[h, 1].wait_recv()
+        up(h, 5, 1, 1, 3)
+        share(h, 3, 0)
+        share(h, 1, 1)
     for h in (0, 1):
         up1[h, 2].wait_recv()
+        share(h, 3, 1)
         up1[h, 3].wait_recv()
-        share(h, 2)
-    for h in (0, 1):
-        lasts[h, 2].wait_recv()
-        store(h, 1 - core, (own[h] + 2) % SIDE)
+        share(h, 1, 0)
+        for n in (0, 1):
+            keep(h, 0, n)
+        keep(h, 3, 0)
+        keep(h, 1, 1)
+    for h in (0, 1):
+        up1[h, 4].wait_recv()
+        share(h, 2, 0)
+        up1[h, 5].wait_recv()
+        share(h, 2, 1)
+    for h in (0, 1):
+        keep(h, 3, 1)
+        keep(h, 1, 0)
+    for h in (0, 1):
+        for n in (0, 1):
+            keep(h, 2, n)
     for group in (pairs, firsts, seconds, deeps, backs, up2, up1, lasts):
         for copy in group.values():
             copy.wait_send()
@@ -341,12 +365,41 @@
         copy.wait()
 
 
+def settle(sources, results, slots, sems):
+    for n, (src, slot) in enumerate(zip(sources, slots)):
+        pltpu.make_async_copy(src, slot, sems.at[0, n]).start()
+    for n, (src, slot, dst) in enumerate(zip(sources, slots, results)):
+        pltpu.make_async_copy(src, slot, sems.at[0, n]).wait()
+        pltpu.make_async_copy(slot, dst, sems.at[1, n]).start()
+    for n, (slot, dst) in enumerate(zip(slots, results)):
+        pltpu.make_async_copy(slot, dst, sems.at[1, n]).wait()
+
+
+def settled(*arrays):
+    def kernel(*refs):
+        count = len(arrays)
+        sources, results, slots, sems = refs[:count], refs[count : 2 * count], refs[2 * count : 3 * count], refs[-1]
+        cuts = [(n, pl.ds(i, a.shape[0] // parts)) for n, (a, parts) in enumerate(zip(arrays, (1, 3, 3)))
+                for i in range(0, a.shape[0], a.shape[0] // parts)]
+        settle(*([refs_[n].at[cut] for n, cut in cuts] for refs_ in (sources, results, slots)), sems)
+
+    hbm = pl.BlockSpec(memory_space=pl.ANY)
+    return pl.pallas_call(
+        kernel,
+        out_shape=tuple(jax.ShapeDtypeStruct(a.shape, a.dtype) for a in arrays),
+        in_specs=[hbm] * len(arrays),
+        out_specs=(hbm,) * len(arrays),
+        scratch_shapes=[pltpu.VMEM(a.shape, a.dtype) for a in arrays] + [pltpu.SemaphoreType.DMA((2, 7))],
+        name="settle",
+    )(*arrays)
+
+
 def per_device(inputs, pre_first, occupancy, grad_out, w_first, w_second):
     size_x, size_y, size_z, chans = inputs.shape
     cells_all = size_x * lax.axis_size("brick") * size_y * size_z * lax.axis_size("slab")
     scale = 10.0 / cells_all**0.5
     dma = pltpu.SemaphoreType.DMA
-    shapes = [(2, 4), (2, 4), (2, 6), (2, 6), (2, 3), (2, 3), (15,), (15,), (15,), (15,), (2, 3), (2, 3), (2, 4), (2, 4), (2, 4), (2, 4)]
+    shapes = [(2, 4), (2, 4), (2, 6), (2, 6), (2, 3), (2, 3), (15,), (15,), (15,), (15,), (2, 3), (2, 3), (2, 6), (2, 6), (2, 4, 2), (2, 4, 2)]
 
     def kernel(*refs):
         body(scale, *refs[:36], refs[36:])
@@ -386,12 +439,12 @@
             pltpu.VMEM((DEPTH - 1, TILE, 128), BF16),
             pltpu.VMEM((DEPTH, TILE, 128), BF16),
             pltpu.VMEM((2, 2, SIDE, PADDED, 128), BF16),
-            dma((6,)), dma((3, 8)), dma((3, 8)), dma((2, 2, SIDE)),
+            dma((6,)), dma((3, 8)), dma((3, 8)), dma((2, 2, SIDE, 2)),
         ] + [dma(s) for s in shapes],
         compiler_params=pltpu.CompilerParams(collective_id=0, has_side_effects=True),
         name="block_backward",
     )(inputs, pre_first, occupancy, grad_out, w_first, w_second)
-    return (grad_in, grad_first.reshape(w_first.shape), grad_second.reshape(w_second.shape))
+    return settled(grad_in, grad_first.reshape(w_first.shape), grad_second.reshape(w_second.shape))
 
 
 def solution(mesh):

time: 83.1 us -> 80.5 us (0.969)
  local copies, waits for them, and re-layouts: 4.74 us -> 0 us
  Pallas kernels: 77.6 us -> 79.6 us
    unnamed x5 -> x0, local copies, waits for them, and re-layouts: 4.74 us -> none
    pallas_call x0 -> x1, Pallas kernels: none -> 2.35 us  [settled(): pl.pallas_call(kernel, out_shape=tuple((jax.ShapeDtypeStruct(a.shape, a.d...]
where the time goes in v4:
time: 80.5 us; the launch traced here: 80.3 us
  Pallas kernels  79.6 us (99%)
    pallas_call x1, Pallas kernels, per_device(): pl.pallas_call(kernel, out_shape=(jax.ShapeDtypeStruct(inputs.shape, BF16...  77.3 us
    pallas_call x1, Pallas kernels, settled(): pl.pallas_call(kernel, out_shape=tuple((jax.ShapeDtypeStruct(a.shape, a.d...  2.35 us

profile of v4, /device:TPU:1, one launch (start us, length us, event | category | flops | bytes accessed | tf_op | source)
XLA Modules:
  0.0 80.3 jit_solution(8936108847894871473)
XLA Ops:
  0.6 77.3 %block_backward.1 = (bf16[4,8,16,128]{3,2,1,0:T(8,128)(2,1)}, bf16[3456,128]{1,0:T(8,128)(2,1)}, bf16[3456,128]{1,0:T(8,128)(2,1)}) custom-call(bf16[4,8,16,128]{3,2,1,0:T(8,128)(2,1)} %refs_0_.1, bf16[4,8,16,128]{3,2,1,0:T(8,128)(2,1)} %refs_1_.1, s32[4,8,16]{2,1,0:T(8,128)} %refs_2_.1, bf16[4,8,16,128]{3,2,1,0:T(8,128)(2,1)} %refs_3_.1, ...), custom_call_target="tpu_custom_call" | custom-call | tf_op jit(solution)/shard_map/block_backward/pallas_call | solution.py:409
  77.9 2.4 %settle.1 = (bf16[4,8,16,128]{3,2,1,0:T(8,128)(2,1)}, bf16[27,128,128]{2,1,0:T(8,128)(2,1)}, bf16[27,128,128]{2,1,0:T(8,128)(2,1)}) custom-call(bf16[4,8,16,128]{3,2,1,0:T(8,128)(2,1)} %get-tuple-element.6.refs_0_, bf16[27,128,128]{2,1,0:T(8,128)(2,1)} %bitcast.2, bf16[27,128,128]{2,1,0:T(8,128)(2,1)} %bitcast.3), custom_call_target="tpu_custom_call" | custom-call | tf_op jit(solution)/shard_map/settle/pallas_call | solution.py:387

commit v5 on v4

--- a/solution.py
+++ b/solution.py
@@ -130,7 +130,6 @@
         for c in (0, 1):
             for i in range(SIDE):
                 part[g, c, i, ROWS:] = jnp.zeros((PADDED - ROWS, 128), BF16)
-    tiles[14:16] = jnp.zeros((2, TILE, 128), BF16)
 
     def mask(i):
         row = occ_in[i].astype(F32)
@@ -249,22 +248,54 @@
             for c in range(3):
                 put(part, 1, k + c, term[:, 128 * c : 128 * c + 128].T)
             start_pairs(1, k // 3)
-    start_firsts(1)
-    start_seconds(0)
-    forward_firsts(1)
-    start_seconds(1)
-    for h in (0, 1):
+    far = sorted(range(1, DEPTH), key=lambda d: -min(d, DEPTH - d))
+    owned = (range(0, 7), range(7, 14))
+
+    def deep_copy(t):
+        slot = (t - z + DEPTH) % DEPTH - 1
+        return send(tiles.at[t], deep_in.at[slot], deep_s.at[t], deep_r.at[slot], device(x, y, t, core))
+
+    def back_copy(d):
+        return send(final.at[z], final.at[z], back_s.at[d], back_r.at[z], deep(d))
+
+    def start_deeps(h):
         for d in (1, 2, 3):
             seconds[h, d].wait_recv()
         total = second_out[h, own[1 - h]].astype(F32)
         for d in (1, 2, 3):
             total = total + second_in[h, d - 1].astype(F32)
         tiles[7 * h : 7 * h + 7] = total.astype(BF16).reshape(7, TILE, 128)
-    far = sorted(range(1, DEPTH), key=lambda d: -min(d, DEPTH - d))
-    deeps = {}
-    for d in far:
-        deeps[d] = send(tiles.at[(z + d) % DEPTH], deep_in.at[d - 1], deep_s.at[d - 1], deep_r.at[d - 1], deep(d))
-        deeps[d].start()
+        for t in owned[h]:
+
+            @pl.when(z != t)
+            def _():
+                deep_copy(t).start()
+
+    def start_backs(h):
+        @pl.when(z // 7 == h)
+        def _():
+            total = tiles[z].astype(F32)
+            for d in reversed(far):
+                send(tiles.at[z], deep_in.at[d - 1], deep_s.at[0], deep_r.at[d - 1], deep(d)).wait_recv()
+                total = total + deep_in[d - 1].astype(F32)
+            final[z] = (total * scale).astype(BF16)
+            for d in far:
+                back_copy(d).start()
+
+    def wait_backs(h):
+        for t in owned[h]:
+
+            @pl.when(z != t)
+            def _():
+                send(final.at[t], final.at[t], back_s.at[0], back_r.at[t], deep(1)).wait_recv()
+
+    start_firsts(1)
+    start_seconds(0)
+    forward_firsts(1)
+    start_deeps(0)
+    start_seconds(1)
+    start_deeps(1)
+    start_backs(0)
 
     for copy in halos[2]:
         copy.wait_recv()
@@ -272,19 +303,10 @@
     back = transpose_conv(ext.at[0], w1)
     grad_in[...] = (grad_out[...].astype(F32) + back.reshape(4, 8, 16, 128)).astype(BF16)
 
-    total = tiles[z].astype(F32)
-    for d in reversed(far):
-        deeps[d].wait_recv()
-        total = total + deep_in[d - 1].astype(F32)
-    final[z] = (total * scale).astype(BF16)
-    backs = {}
-    for d in far:
-        backs[d] = send(final.at[z], final.at[z], back_s.at[d - 1], back_r.at[d - 1], deep(d))
-        backs[d].start()
-    for d in reversed(far):
-        backs[d].wait_recv()
+    start_backs(1)
     up2 = {}
     for h in (0, 1):
+        wait_backs(h)
         rows = pl.ds(pl.multiple_of(own[1 - h] * PIECE, PIECE), PIECE)
         out[h, core, own[h], rows] = final[7 * h : 7 * h + 7].reshape(PIECE, 128)
         place = out.at[h, core, own[h], rows]
@@ -319,7 +341,7 @@
         lasts[h, came, n].wait_recv()
         store(h, 1 - core, (own[h] + came) % SIDE, n)
 
-    for h in (0, 1):
+    def own_chunk(h):
         for d in (1, 2, 3):
             up2[h, d].wait_recv()
         up(h, 0, 0, 0, 1)
@@ -328,14 +350,16 @@
         up(h, 3, 0, 0, 3)
         share(h, 0, 0)
         share(h, 0, 1)
-    for h in (0, 1):
+
+    def forward(h):
         up1[h, 0].wait_recv()
         up(h, 4, 3, 0, 1)
         up1[h, 1].wait_recv()
         up(h, 5, 1, 1, 3)
         share(h, 3, 0)
         share(h, 1, 1)
-    for h in (0, 1):
+
+    def others(h):
         up1[h, 2].wait_recv()
         share(h, 3, 1)
         up1[h, 3].wait_recv()
@@ -344,18 +368,41 @@
             keep(h, 0, n)
         keep(h, 3, 0)
         keep(h, 1, 1)
-    for h in (0, 1):
+
+    def opposite(h):
         up1[h, 4].wait_recv()
         share(h, 2, 0)
         up1[h, 5].wait_recv()
         share(h, 2, 1)
-    for h in (0, 1):
+
+    def rest(h):
         keep(h, 3, 1)
         keep(h, 1, 0)
-    for h in (0, 1):
         for n in (0, 1):
             keep(h, 2, n)
-    for group in (pairs, firsts, seconds, deeps, backs, up2, up1, lasts):
+
+    own_chunk(0)
+    forward(0)
+    own_chunk(1)
+    others(0)
+    forward(1)
+    opposite(0)
+    others(1)
+    opposite(1)
+    rest(0)
+    rest(1)
+    for t in range(14):
+
+        @pl.when(z != t)
+        def _():
+            deep_copy(t).wait_send()
+
+    @pl.when(z < 14)
+    def _():
+        for d in range(1, DEPTH):
+            back_copy(d).wait_send()
+
+    for group in (pairs, firsts, seconds, up2, up1, lasts):
         for copy in group.values():
             copy.wait_send()
     for copies in halos:
@@ -399,7 +446,7 @@
     cells_all = size_x * lax.axis_size("brick") * size_y * size_z * lax.axis_size("slab")
     scale = 10.0 / cells_all**0.5
     dma = pltpu.SemaphoreType.DMA
-    shapes = [(2, 4), (2, 4), (2, 6), (2, 6), (2, 3), (2, 3), (15,), (15,), (15,), (15,), (2, 3), (2, 3), (2, 6), (2, 6), (2, 4, 2), (2, 4, 2)]
+    shapes = [(2, 4), (2, 4), (2, 6), (2, 6), (2, 3), (2, 3), (16,), (16,), (16,), (16,), (2, 3), (2, 3), (2, 6), (2, 6), (2, 4, 2), (2, 4, 2)]
 
     def kernel(*refs):
         body(scale, *refs[:36], refs[36:])

time: 80.5 us -> 80.3 us (level)
  no operation moved by 1% of the time
where the time goes in v5:
time: 80.3 us; the launch traced here: 80.1 us
  Pallas kernels  79.5 us (99%)
    pallas_call x1, Pallas kernels, per_device(): pl.pallas_call(kernel, out_shape=(jax.ShapeDtypeStruct(inputs.shape, BF16...  77.2 us
    pallas_call x1, Pallas kernels, settled(): pl.pallas_call(kernel, out_shape=tuple((jax.ShapeDtypeStruct(a.shape, a.d...  2.35 us

profile of v5, /device:TPU:1, one launch (start us, length us, event | category | flops | bytes accessed | tf_op | source)
XLA Modules:
  0.0 80.1 jit_solution(15487763079643473089)
XLA Ops:
  0.6 77.2 %block_backward.1 = (bf16[4,8,16,128]{3,2,1,0:T(8,128)(2,1)}, bf16[3456,128]{1,0:T(8,128)(2,1)}, bf16[3456,128]{1,0:T(8,128)(2,1)}) custom-call(bf16[4,8,16,128]{3,2,1,0:T(8,128)(2,1)} %refs_0_.1, bf16[4,8,16,128]{3,2,1,0:T(8,128)(2,1)} %refs_1_.1, s32[4,8,16]{2,1,0:T(8,128)} %refs_2_.1, bf16[4,8,16,128]{3,2,1,0:T(8,128)(2,1)} %refs_3_.1, ...), custom_call_target="tpu_custom_call" | custom-call | tf_op jit(solution)/shard_map/block_backward/pallas_call | solution.py:456
  77.8 2.4 %settle.1 = (bf16[4,8,16,128]{3,2,1,0:T(8,128)(2,1)}, bf16[27,128,128]{2,1,0:T(8,128)(2,1)}, bf16[27,128,128]{2,1,0:T(8,128)(2,1)}) custom-call(bf16[4,8,16,128]{3,2,1,0:T(8,128)(2,1)} %get-tuple-element.6.refs_0_, bf16[27,128,128]{2,1,0:T(8,128)(2,1)} %bitcast.2, bf16[27,128,128]{2,1,0:T(8,128)(2,1)} %bitcast.3), custom_call_target="tpu_custom_call" | custom-call | tf_op jit(solution)/shard_map/settle/pallas_call | solution.py:434

commit v6 on v5

--- a/solution.py
+++ b/solution.py
@@ -153,7 +153,10 @@
     lax.fori_loop(0, 4, masked, 0)
     pl.semaphore_wait(barrier, len(everyone))
 
-    halos = [exchange(bases.at[f], faces.at[f], zins.at[f], halo_s.at[f], halo_r.at[f]) for f in (0, 1)]
+    def start_halo(f):
+        return exchange(bases.at[f], faces.at[f], zins.at[f], halo_s.at[f], halo_r.at[f])
+
+    halos = [start_halo(0)]
 
     def pointwise(i, carry):
         v, occ = pre[i].astype(F32), mask(i)
@@ -164,6 +167,7 @@
 
     loads[3].wait()
     lax.fori_loop(0, 4, pointwise, 0)
+    halos.append(start_halo(1))
     act_t = act[...].reshape(512, 128).T
     loads[4].wait()
     loads[5].wait()
@@ -234,7 +238,7 @@
     wide = grad_pre.astype(F32)
     faces[2, 0] = wide[:, :, 15, :].astype(BF16)
     faces[2, 1] = wide[:, :, 0, :].astype(BF16)
-    halos.append(exchange(bases.at[2], faces.at[2], zins.at[2], halo_s.at[2], halo_r.at[2]))
+    halos.append(start_halo(2))
     start_firsts(0)
     for copy in halos[1]:
         copy.wait_recv()

time: 80.3 us -> 80.7 us (level)
  no operation moved by 1% of the time
where the time goes in v6:
time: 80.7 us; the launch traced here: 80.6 us
  Pallas kernels  79.9 us (99%)
    pallas_call x1, Pallas kernels, per_device(): pl.pallas_call(kernel, out_shape=(jax.ShapeDtypeStruct(inputs.shape, BF16...  77.6 us
    pallas_call x1, Pallas kernels, settled(): pl.pallas_call(kernel, out_shape=tuple((jax.ShapeDtypeStruct(a.shape, a.d...  2.35 us

profile of v6, /device:TPU:1, one launch (start us, length us, event | category | flops | bytes accessed | tf_op | source)
XLA Modules:
  0.0 80.6 jit_solution(4011978294258892313)
XLA Ops:
  0.6 77.6 %block_backward.1 = (bf16[4,8,16,128]{3,2,1,0:T(8,128)(2,1)}, bf16[3456,128]{1,0:T(8,128)(2,1)}, bf16[3456,128]{1,0:T(8,128)(2,1)}) custom-call(bf16[4,8,16,128]{3,2,1,0:T(8,128)(2,1)} %refs_0_.1, bf16[4,8,16,128]{3,2,1,0:T(8,128)(2,1)} %refs_1_.1, s32[4,8,16]{2,1,0:T(8,128)} %refs_2_.1, bf16[4,8,16,128]{3,2,1,0:T(8,128)(2,1)} %refs_3_.1, ...), custom_call_target="tpu_custom_call" | custom-call | tf_op jit(solution)/shard_map/block_backward/pallas_call | solution.py:460
  78.2 2.4 %settle.1 = (bf16[4,8,16,128]{3,2,1,0:T(8,128)(2,1)}, bf16[27,128,128]{2,1,0:T(8,128)(2,1)}, bf16[27,128,128]{2,1,0:T(8,128)(2,1)}) custom-call(bf16[4,8,16,128]{3,2,1,0:T(8,128)(2,1)} %get-tuple-element.6.refs_0_, bf16[27,128,128]{2,1,0:T(8,128)(2,1)} %bitcast.2, bf16[27,128,128]{2,1,0:T(8,128)(2,1)} %bitcast.3), custom_call_target="tpu_custom_call" | custom-call | tf_op jit(solution)/shard_map/settle/pallas_call | solution.py:438
